TPU v7x, 32 devices: a whole 2x2x4 slice. The times are simulated.
32 devices in a mesh: shard: 4 (over y, x), ctx: 4 (over z), tp: 2 (over core).
Axes of the slice: x: 2, y: 2, z: 4, core: 2. Of those that a mesh axis runs over, the one named last changes fastest.
Arguments:
- inputs: bfloat16 [4096, 1024], P(('shard', 'ctx')), may hold values from -6 to 6
- lengths: int32 [4, 3], P('shard'), may hold values from 1 to 768, 1024 in all within a row
- cotangent: bfloat16 [4096, 1024], P(('shard', 'ctx')), may hold values from -6 to 6
- w_qkv: bfloat16 [3, 1024, 1024], P(None, 'shard', 'tp'), may hold values from -0.1875 to 0.1875
- w_out: bfloat16 [1024, 1024], P('tp', 'shard'), may hold values from -0.5 to 0.5
- w_fc: bfloat16 [1024, 4096], P('shard', 'tp'), may hold values from -0.1875 to 0.1875
- w_proj: bfloat16 [4096, 1024], P('tp', 'shard'), may hold values from -0.09375 to 0.09375
- b_qv: float32 [2, 1024], P(None, 'tp'), may hold values from -3 to 3
- b_out: float32 [1024], replicated, may hold values from -2 to 2
- b_fc: float32 [4096], P('tp'), may hold values from -3 to 3
- b_proj: float32 [1024], replicated, may hold values from -2 to 2
- ln1_gain: float32 [1024], replicated, may hold values from 0.25 to 1.75
- ln1_bias: float32 [1024], replicated, may hold values from -2 to 2
- ln2_gain: float32 [1024], replicated, may hold values from 0.25 to 1.75
- ln2_bias: float32 [1024], replicated, may hold values from -2 to 2
Outputs:
- outputs: bfloat16 [4096, 1024], P(('shard', 'ctx'))
- grad_inputs: bfloat16 [4096, 1024], P(('shard', 'ctx'))
- grad_w_qkv: float32 [3, 1024, 1024], P(None, 'shard', 'tp')
- grad_w_out: float32 [1024, 1024], P('tp', 'shard')
- grad_w_fc: float32 [1024, 4096], P('shard', 'tp')
- grad_w_proj: float32 [4096, 1024], P('tp', 'shard')
- grad_b_qv: float32 [2, 1024], P(None, 'tp')
- grad_b_out: float32 [1024], replicated
- grad_b_fc: float32 [4096], P('tp')
- grad_b_proj: float32 [1024], replicated
- grad_ln1_gain: float32 [1024], replicated
- grad_ln1_bias: float32 [1024], replicated
- grad_ln2_gain: float32 [1024], replicated
- grad_ln2_bias: float32 [1024], replicated
Inputs may be any that keep to these rules, and one draw needn't show every extreme that they name: Each row holds the lengths of one shard's 3 sequences in order; they sum to 1024, and the largest is 768.
All inputs are finite; a program needn't handle non-finite values.
Results may differ from a plain program's by a relative error of at most 0.02.
Values may be sent and summed in bfloat16 or wider, within the bound.
A program may use at most 128 MiB of HBM per device.

v0:
```python
import jax
import jax.numpy as jnp
from jax import lax
from jax.sharding import PartitionSpec as P

HEAD_DIM = 64


def layer_norm(values, gain, shift):
    mean = jnp.mean(values, axis=-1, keepdims=True)
    centred = values - mean
    spread = jnp.mean(centred * centred, axis=-1, keepdims=True)
    return centred * lax.rsqrt(spread + 1e-05) * gain + shift


def gelu_tanh(values):
    return (
        0.5
        * values
        * (1.0 + jnp.tanh(0.7978845608028654 * (values + 0.044715 * values * values * values)))
    )


def segment_ids(lengths, count):
    ends = jnp.cumsum(lengths)
    places = jnp.arange(count, dtype=jnp.int32)
    return jnp.sum((places[:, None] >= ends[None, :]).astype(jnp.int32), axis=1)


def dot32(left, right):
    return jnp.dot(left, right, preferred_element_type=jnp.float32)


def on_device(
    inputs,
    lengths,
    cotangent,
    w_qkv,
    w_out,
    w_fc,
    w_proj,
    b_qv,
    b_out,
    b_fc,
    b_proj,
    ln1_gain,
    ln1_bias,
    ln2_gain,
    ln2_bias,
):
    bf = jnp.bfloat16
    f32 = jnp.float32
    rows = inputs.shape[0]
    parts = lax.axis_size("ctx")
    block = rows * parts
    local_width = b_qv.shape[1]
    local_heads = local_width // HEAD_DIM
    seg_all = segment_ids(lengths[0], block)
    first = lax.axis_index("ctx") * rows
    q_pos = first + jnp.arange(rows, dtype=jnp.int32)
    q_seg = lax.dynamic_slice_in_dim(seg_all, first, rows)
    wq_all, wo_all, wfc_all, wproj_all = (
        lax.all_gather(w_qkv, "shard", axis=1, tiled=True),
        lax.all_gather(w_out, "shard", axis=1, tiled=True),
        lax.all_gather(w_fc, "shard", axis=0, tiled=True),
        lax.all_gather(w_proj, "shard", axis=1, tiled=True),
    )
    x_f = inputs.astype(f32)
    normed1 = layer_norm(x_f, ln1_gain, ln1_bias).astype(bf)
    query = ((dot32(normed1, wq_all[0]) + b_qv[0]) * 0.125).astype(bf)
    key = dot32(normed1, wq_all[1]).astype(bf)
    value = (dot32(normed1, wq_all[2]) + b_qv[1]).astype(bf)
    q3 = query.reshape(rows, local_heads, HEAD_DIM)

    def allowed_for(start, count):
        k_pos = start + jnp.arange(count, dtype=jnp.int32)
        k_seg = lax.dynamic_slice_in_dim(seg_all, start, count)
        return (k_pos[None, :] <= q_pos[:, None]) & (k_seg[None, :] == q_seg[:, None])

    k_piece = lax.all_gather(key, "ctx", axis=0, tiled=True)
    v_piece = lax.all_gather(value, "ctx", axis=0, tiled=True)
    count = k_piece.shape[0]
    allowed = allowed_for(jnp.int32(0), count)
    scores = jnp.einsum(
        "rhd,nhd->hrn",
        q3,
        k_piece.reshape(count, local_heads, HEAD_DIM),
        preferred_element_type=f32,
    )
    weights = jnp.where(allowed[None], jnp.exp(scores), 0.0)
    total = jnp.sum(weights, axis=2)
    acc = jnp.einsum(
        "hrn,nhd->hrd",
        weights.astype(bf),
        v_piece.reshape(count, local_heads, HEAD_DIM),
        preferred_element_type=f32,
    )
    total, acc = (total, acc)
    log_total = jnp.log(total)
    attended = (acc / total[:, :, None]).transpose(1, 0, 2).reshape(rows, local_width).astype(bf)
    mixed = lax.psum(dot32(attended, wo_all).astype(jnp.bfloat16), "tp").astype(jnp.float32)
    hidden = x_f + mixed + b_out
    normed2 = layer_norm(hidden, ln2_gain, ln2_bias).astype(bf)
    pre = dot32(normed2, wfc_all) + b_fc
    act = gelu_tanh(pre).astype(bf)
    mlp_total = lax.psum(dot32(act, wproj_all).astype(jnp.bfloat16), "tp").astype(jnp.float32)
    outputs = (hidden + mlp_total + b_proj).astype(bf)
    wq_back, wo_back, wfc_back, wproj_back = (
        lax.all_gather(w_qkv, "shard", axis=1, tiled=True),
        lax.all_gather(w_out, "shard", axis=1, tiled=True),
        lax.all_gather(w_fc, "shard", axis=0, tiled=True),
        lax.all_gather(w_proj, "shard", axis=1, tiled=True),
    )
    grad_f = cotangent.astype(f32)
    g_bproj = jnp.sum(grad_f, axis=0)
    g_proj = dot32(act.T, cotangent)
    d_act = dot32(cotangent, wproj_back.T)
    gelu_back = jax.vjp(gelu_tanh, pre)[1]
    d_pre = gelu_back(d_act)[0]
    g_bfc = jnp.sum(d_pre, axis=0)
    d_pre_b = d_pre.astype(bf)
    g_fc = dot32(normed2.T, d_pre_b)
    d_normed2 = lax.psum(dot32(d_pre_b, wfc_back.T).astype(jnp.bfloat16), "tp").astype(jnp.float32)
    norm_back2 = jax.vjp(layer_norm, hidden, ln2_gain, ln2_bias)[1]
    d_norm2, g_ln2g, g_ln2b = norm_back2(d_normed2)
    d_hidden = grad_f + d_norm2
    g_bout = jnp.sum(d_hidden, axis=0)
    d_hidden_b = d_hidden.astype(bf)
    g_out = dot32(attended.T, d_hidden_b)
    d_attended = dot32(d_hidden_b, wo_back.T).astype(bf)
    da3 = d_attended.reshape(rows, local_heads, HEAD_DIM)
    at3 = attended.reshape(rows, local_heads, HEAD_DIM)
    delta = jnp.einsum("rhd,rhd->hr", da3, at3, preferred_element_type=f32)
    key_all, value_all = (
        lax.all_gather(key, "ctx", axis=0, tiled=True),
        lax.all_gather(value, "ctx", axis=0, tiled=True),
    )
    key_blocks = key_all.reshape(parts, rows, local_heads, HEAD_DIM)
    value_blocks = value_all.reshape(parts, rows, local_heads, HEAD_DIM)
    starts = jnp.arange(parts, dtype=jnp.int32) * rows

    def back_piece(d_query_acc, inputs_piece):
        k_piece, v_piece, start = inputs_piece
        allowed = allowed_for(start, rows)
        scores = jnp.einsum("rhd,nhd->hrn", q3, k_piece, preferred_element_type=f32)
        probs = jnp.where(allowed[None], jnp.exp(scores - log_total[:, :, None]), 0.0)
        d_v = jnp.einsum("hrn,rhd->nhd", probs.astype(bf), da3, preferred_element_type=f32)
        d_probs = jnp.einsum("rhd,nhd->hrn", da3, v_piece, preferred_element_type=f32)
        d_scores_b = (probs * (d_probs - delta[:, :, None])).astype(bf)
        d_query_acc = d_query_acc + jnp.einsum(
            "hrn,nhd->rhd", d_scores_b, k_piece, preferred_element_type=f32
        )
        d_k = jnp.einsum("hrn,rhd->nhd", d_scores_b, q3, preferred_element_type=f32)
        return (d_query_acc, (d_k.reshape(rows, local_width), d_v.reshape(rows, local_width)))

    zero_query = jnp.zeros((rows, local_heads, HEAD_DIM), f32)
    d_query_acc, (d_key_terms, d_value_terms) = lax.scan(
        back_piece, zero_query, (key_blocks, value_blocks, starts)
    )
    d_key, d_value = (
        lax.psum_scatter(
            d_key_terms.reshape(block, local_width).astype(jnp.bfloat16),
            "ctx",
            scatter_dimension=0,
            tiled=True,
        ).astype(jnp.float32),
        lax.psum_scatter(
            d_value_terms.reshape(block, local_width).astype(jnp.bfloat16),
            "ctx",
            scatter_dimension=0,
            tiled=True,
        ).astype(jnp.float32),
    )
    d_query = d_query_acc.reshape(rows, local_width) * 0.125
    g_bqv = jnp.stack([jnp.sum(d_query, axis=0), jnp.sum(d_value, axis=0)])
    d_query_b = d_query.astype(bf)
    d_key_b = d_key.astype(bf)
    d_value_b = d_value.astype(bf)
    g_qkv = jnp.stack(
        [dot32(normed1.T, d_query_b), dot32(normed1.T, d_key_b), dot32(normed1.T, d_value_b)]
    )
    d_local = (
        dot32(d_query_b, wq_back[0].T)
        + dot32(d_key_b, wq_back[1].T)
        + dot32(d_value_b, wq_back[2].T)
    )
    d_normed1 = lax.psum(d_local.astype(jnp.bfloat16), "tp").astype(jnp.float32)
    norm_back1 = jax.vjp(layer_norm, x_f, ln1_gain, ln1_bias)[1]
    d_norm1, g_ln1g, g_ln1b = norm_back1(d_normed1)
    grad_inputs = (d_hidden + d_norm1).astype(bf)
    part_qkv, part_out, part_fc, part_proj = (
        lax.psum_scatter(
            g_qkv.astype(jnp.bfloat16), "shard", scatter_dimension=1, tiled=True
        ).astype(jnp.float32),
        lax.psum_scatter(
            g_out.astype(jnp.bfloat16), "shard", scatter_dimension=1, tiled=True
        ).astype(jnp.float32),
        lax.psum_scatter(
            g_fc.astype(jnp.bfloat16), "shard", scatter_dimension=0, tiled=True
        ).astype(jnp.float32),
        lax.psum_scatter(
            g_proj.astype(jnp.bfloat16), "shard", scatter_dimension=1, tiled=True
        ).astype(jnp.float32),
    )
    sum_qkv, sum_out, sum_fc, sum_proj = (
        lax.psum(part_qkv.astype(jnp.bfloat16), "ctx").astype(jnp.float32),
        lax.psum(part_out.astype(jnp.bfloat16), "ctx").astype(jnp.float32),
        lax.psum(part_fc.astype(jnp.bfloat16), "ctx").astype(jnp.float32),
        lax.psum(part_proj.astype(jnp.bfloat16), "ctx").astype(jnp.float32),
    )
    small = lax.psum(
        (g_bqv, g_bout, g_bfc, g_bproj, g_ln1g, g_ln1b, g_ln2g, g_ln2b), ("shard", "ctx")
    )
    return (
        outputs,
        grad_inputs,
        sum_qkv,
        sum_out,
        sum_fc,
        sum_proj,
        small[0],
        small[1],
        small[2],
        small[3],
        small[4],
        small[5],
        small[6],
        small[7],
    )


def solution(mesh):
    in_specs = (
        P(("shard", "ctx"), None),
        P("shard", None),
        P(("shard", "ctx"), None),
        P(None, "shard", "tp"),
        P("tp", "shard"),
        P("shard", "tp"),
        P("tp", "shard"),
        P(None, "tp"),
        P(),
        P("tp"),
        P(),
        P(),
        P(),
        P(),
        P(),
    )
    out_specs = (
        P(("shard", "ctx"), None),
        P(("shard", "ctx"), None),
        P(None, "shard", "tp"),
        P("tp", "shard"),
        P("shard", "tp"),
        P("tp", "shard"),
        P(None, "tp"),
        P(),
        P("tp"),
        P(),
        P(),
        P(),
        P(),
        P(),
    )
    return jax.shard_map(
        on_device, mesh=mesh, in_specs=in_specs, out_specs=out_specs, check_vma=False
    )
```

profile of v0, /device:TPU:0, one launch (start us, length us, event | category | flops | bytes accessed | tf_op | source)
XLA Modules:
  0.0 772.6 jit_solution(15052894565088602509)
XLA Ops:
  11.4 45.1 %all-gather.7.cloned.1.call-done = bf16[3,1024,512]{2,1,0:T(8,128)(2,1)} async-done(((bf16[3,256,512]{2,1,0:T(8,128)(2,1)}), bf16[3,1024,512]{2,1,0:T(8,128)(2,1)}) %all-gather.7.cloned.1.call-update) | async-done | bytes 3145744 | tf_op jit(solution)/shard_map/all_gather | solution.py:63
  64.8 22.4 %all-gather.11.cloned.1.call-done = bf16[1024,512]{1,0:T(8,128)(2,1)} async-done(((bf16[256,512]{1,0:T(8,128)(2,1)}), bf16[1024,512]{1,0:T(8,128)(2,1)}) %all-gather.11.cloned.1.call-update) | async-done | bytes 1048592 | tf_op jit(solution)/shard_map/all_gather | solution.py:81
  88.7 28.1 %all-gather.9.cloned.1.call-done = bf16[1024,512]{1,0:T(8,128)(2,1)} async-done(((bf16[256,512]{1,0:T(8,128)(2,1)}), bf16[1024,512]{1,0:T(8,128)(2,1)}) %all-gather.9.cloned.1.call-update) | async-done | bytes 1048592 | tf_op jit(solution)/shard_map/all_gather | solution.py:80
  121.7 22.5 %all-gather.13.cloned.1.call-done = bf16[512,1024]{1,0:T(8,128)(2,1)} async-done(((bf16[512,256]{1,0:T(8,128)(2,1)}), bf16[512,1024]{1,0:T(8,128)(2,1)}) %all-gather.13.cloned.1.call-update) | async-done | bytes 1048592 | tf_op jit(solution)/shard_map/all_gather | solution.py:64
  148.2 17.4 %all-reduce.8.cloned.1.call-done = bf16[256,1024]{1,0:T(8,128)(2,1)} async-done(((bf16[256,1024]{1,0:T(8,128)(2,1)}), bf16[256,1024]{1,0:T(8,128)(2,1)}) %all-reduce.8.cloned.1.call-update) | async-done | bytes 524304 | tf_op jit(solution)/shard_map/psum | solution.py:101
  168.4 52.8 %all-gather.15.cloned.1.call-done = bf16[1024,2048]{1,0:T(8,128)(2,1)} async-done(((bf16[256,2048]{1,0:T(8,128)(2,1)}), bf16[1024,2048]{1,0:T(8,128)(2,1)}) %all-gather.15.cloned.1.call-update) | async-done | bytes 4194320 | tf_op jit(solution)/shard_map/all_gather | solution.py:65
  221.1 4.9 convolution_add_fusion
  226.0 49.4 %all-gather.17.cloned.1.call-done = bf16[2048,1024]{1,0:T(8,128)(2,1)} async-done(((bf16[2048,256]{1,0:T(8,128)(2,1)}), bf16[2048,1024]{1,0:T(8,128)(2,1)}) %all-gather.17.cloned.1.call-update) | async-done | bytes 4194320 | tf_op jit(solution)/shard_map/all_gather | solution.py:66
  275.4 7.6 fusion.86
  291.2 2.8 reshape.279
  295.9 9.0 %all-reduce.10.cloned.1.call-done = bf16[256,1024]{1,0:T(8,128)(2,1)} async-done(((bf16[256,1024]{1,0:T(8,128)(2,1)}), bf16[256,1024]{1,0:T(8,128)(2,1)}) %all-reduce.10.cloned.1.call-update) | async-done | bytes 524304 | tf_op jit(solution)/shard_map/psum | solution.py:123
  312.3 53.9 %while.15 = (s32[]{:T(128)}, f32[256,8,64]{0,2,1:T(8,128)}, bf16[4,256,512]{2,1,0:T(8,128)(2,1)}, bf16[4,256,512]{2,1,0:T(8,128)(2,1)}, bf16[4,256,8,64]{1,3,2,0...) while((s32[]{:T(128)}, f32[256,8,64]{0,2,1:T(8,128)}, ...), condition=%wide.region_13.14_spmd.clone, body=%wide.region_12.13_spmd.clone.sunk | while | flops 340197888 | bytes 15172017 | solution.py:157
  368.9 3.4 convolution_convert_fusion.1
  373.4 5.2 convolution_convert_fusion
  381.4 13.5 %reduce-scatter.9.cloned.1.call-done = bf16[256,512]{1,0:T(8,128)(2,1)} async-done(((bf16[1024,512]{1,0:T(8,128)(2,1)}), bf16[256,512]{1,0:T(8,128)(2,1)}) %reduce-scatter.9.cloned.1.call-update) | async-done | bytes 262160 | tf_op jit(solution)/shard_map/reduce_scatter | solution.py:167
  397.4 26.0 %reduce-scatter.7.cloned.1.call-done = bf16[256,512]{1,0:T(8,128)(2,1)} async-done(((bf16[1024,512]{1,0:T(8,128)(2,1)}), bf16[256,512]{1,0:T(8,128)(2,1)}) %reduce-scatter.7.cloned.1.call-update) | async-done | bytes 262160 | tf_op jit(solution)/shard_map/reduce_scatter | solution.py:161
  427.2 5.2 convolution_convert_fusion.8
  435.7 17.1 %reduce-scatter.13.cloned.1.call-done = bf16[512,256]{1,0:T(8,128)(2,1)} async-done(((bf16[512,1024]{1,0:T(8,128)(2,1)}), bf16[512,256]{1,0:T(8,128)(2,1)}) %reduce-scatter.13.cloned.1.call-update) | async-done | bytes 262160 | tf_op jit(solution)/shard_map/reduce_scatter | solution.py:195
  452.8 55.4 %reduce-scatter.15.cloned.1.call-done = bf16[256,2048]{1,0:T(8,128)(2,1)} async-done(((bf16[1024,2048]{1,0:T(8,128)(2,1)}), bf16[256,2048]{1,0:T(8,128)(2,1)}) %reduce-scatter.15.cloned.1.call-update) | async-done | bytes 1048592 | tf_op jit(solution)/shard_map/reduce_scatter | solution.py:198
  508.2 55.6 %reduce-scatter.17.cloned.1.call-done = bf16[2048,256]{1,0:T(8,128)(2,1)} async-done(((bf16[2048,1024]{1,0:T(8,128)(2,1)}), bf16[2048,256]{1,0:T(8,128)(2,1)}) %reduce-scatter.17.cloned.1.call-update) | async-done | bytes 1048592 | tf_op jit(solution)/shard_map/reduce_scatter | solution.py:201
  563.8 46.8 %reduce-scatter.11.cloned.1.call-done = bf16[3,256,512]{2,1,0:T(8,128)(2,1)} async-done(((bf16[3,1024,512]{2,1,0:T(8,128)(2,1)}), bf16[3,256,512]{2,1,0:T(8,128)(2,1)}) %reduce-scatter.11.cloned.1.call-update) | async-done | bytes 786448 | tf_op jit(solution)/shard_map/reduce_scatter | solution.py:192
  610.8 22.1 %all-reduce.14.cloned.1.call-done = (bf16[256,1024]{1,0:T(8,128)(2,1)}, bf16[256,1024]{1,0:T(8,128)(2,1)}) async-done(((bf16[256,1024]{1,0:T(8,128)(2,1)}, bf16[256,1024]{1,0:T(8,128)(2,1)}), (bf16[256,1024]{1,0:T(8,128)(2,1)}, bf16[256,1024]{1,0:T(8,128)(2,1)})) %all-reduce.14.cloned.1.call-update) | async-done | bytes 1048592 | tf_op jit(solution)/shard_map/psum | solution.py:106
  636.1 82.1 %all-reduce = (f32[2,512]{1,0:T(2,128)}, f32[1024]{0:T(1024)}, f32[2048]{0:T(1024)}, f32[1024]{0:T(1024)}, f32[1024]{0:T(1024)}, /*index=5*/f32[1024]{0:T(1024)}, f32[1024]{0:T(1024)}, f32[1024]{0:T(1024)}) all-reduce(f32[2,512]{1,0:T(2,128)S(1)} %pad_maximum_fusion.1, ...), channel_id=1, replica_groups=mesh['shard'=4,'ctx'=4,'tp'=2] {'shard','ctx'}, use_global_device_ids=true, to_apply=%region_29.30 | all-reduce | flops 9216 | bytes 73728 | tf_op jit(solution)/shard_map/psum | solution.py:211
  719.7 39.9 %all-reduce.12.cloned.1.call-done = (bf16[3,256,512]{2,1,0:T(8,128)(2,1)}, bf16[512,256]{1,0:T(8,128)(2,1)}, bf16[256,2048]{1,0:T(8,128)(2,1)}, bf16[2048,256]{1,0:T(8,128)(2,1)}) async-done(((bf16[3,256,512]{2,1,0:T(8,128)(2,1)}, bf16[512,256]{1,0:T(8,128)(2,1)}, bf16[256,2048]{1,0:T(8,128)(2,1)}, bf16[2048,256]{1,0:T(8,128)(2,1)}), (bf16[3,256,512]{2,1,0:T(8,128)(2,1)}, bf16[512,256]{1,0:T(8,128)(2,1)}, ...) | async-done | bytes 3145744 | tf_op jit(solution)/shard_map/psum | solution.py:206
  (235 shorter events, 116.0 us)
Async XLA Ops:
  7.2 49.3 %all-gather.7.cloned.1.call-start = ((), (), s32[]{:S(2)}) async-start(), calls=%async_computation.6 | async-start | bytes 3932160 | tf_op jit(solution)/shard_map/all_gather | solution.py:63
  7.9 79.3 %all-gather.11.cloned.1.call-start = ((), (), s32[]{:S(2)}) async-start(), calls=%async_computation.8 | async-start | bytes 1310720 | tf_op jit(solution)/shard_map/all_gather | solution.py:81
  59.1 57.7 %all-gather.9.cloned.1.call-start = ((), (), s32[]{:S(2)}) async-start(), calls=%async_computation.7 | async-start | bytes 1310720 | tf_op jit(solution)/shard_map/all_gather | solution.py:80
  61.6 82.6 %all-gather.13.cloned.1.call-start = ((), (), s32[]{:S(2)}) async-start(), calls=%async_computation.9 | async-start | bytes 1310720 | tf_op jit(solution)/shard_map/all_gather | solution.py:64
  62.2 103.4 %all-reduce.8.cloned.1.call-start = ((), (), s32[]{:S(2)}) async-start(), calls=%async_computation.10 | async-start | bytes 1048576 | tf_op jit(solution)/shard_map/psum | solution.py:101
  146.7 74.4 %copy-start.28 = (f32[1024]{0:T(1024)S(1)}, f32[1024]{0:T(1024)}, u32[]{:S(2)}) copy-start(f32[1024]{0:T(1024)} %param.30) | copy-start | bytes 12292
  146.8 74.4 %copy-start.29 = (f32[1024]{0:T(1024)S(1)}, f32[1024]{0:T(1024)}, u32[]{:S(2)}) copy-start(f32[1024]{0:T(1024)} %param.31) | copy-start | bytes 12292
  146.8 74.4 %copy-start.34 = (f32[2048]{0:T(1024)S(1)}, f32[2048]{0:T(1024)}, u32[]{:S(2)}) copy-start(f32[2048]{0:T(1024)} %param.26) | copy-start | bytes 24580
  146.8 74.3 %all-gather.15.cloned.1.call-start = ((), (), s32[]{:S(2)}) async-start(), calls=%async_computation.11 | async-start | bytes 5242880 | tf_op jit(solution)/shard_map/all_gather | solution.py:65
  147.4 128.1 %all-gather.17.cloned.1.call-start = ((), (), s32[]{:S(2)}) async-start(), calls=%async_computation.12 | async-start | bytes 5242880 | tf_op jit(solution)/shard_map/all_gather | solution.py:66
  148.1 156.8 %all-reduce.10.cloned.1.call-start = ((), (), s32[]{:S(2)}) async-start(), calls=%async_computation.13 | async-start | bytes 1048576 | tf_op jit(solution)/shard_map/psum | solution.py:123
  165.6 55.5 %copy-start.2 = (bf16[256,1024]{1,0:T(8,128)(2,1)S(1)}, bf16[256,1024]{1,0:T(8,128)(2,1)}, u32[]{:S(2)}) copy-start(bf16[256,1024]{1,0:T(8,128)(2,1)} %all-reduce.8.cloned.1.call-done) | copy-start | bytes 1572868
  168.4 107.1 %copy-start.21 = (bf16[256,1024]{1,0:T(8,128)(2,1)S(1)}, bf16[256,1024]{1,0:T(8,128)(2,1)}, u32[]{:S(2)}) copy-start(bf16[256,1024]{1,0:T(8,128)(2,1)} %param.19) | copy-start | bytes 1572868
  286.2 108.7 %reduce-scatter.9.cloned.1.call-start = ((), (), s32[]{:S(2)}) async-start(), calls=%async_computation.15 | async-start | bytes 1310720 | tf_op jit(solution)/shard_map/reduce_scatter | solution.py:167
  366.2 57.2 %reduce-scatter.7.cloned.1.call-start = ((), (), s32[]{:S(2)}) async-start(), calls=%async_computation.14 | async-start | bytes 1310720 | tf_op jit(solution)/shard_map/reduce_scatter | solution.py:161
  366.8 86.0 %reduce-scatter.13.cloned.1.call-start = ((), (), s32[]{:S(2)}) async-start(), calls=%async_computation.17 | async-start | bytes 1310720 | tf_op jit(solution)/shard_map/reduce_scatter | solution.py:195
  368.9 139.3 %reduce-scatter.15.cloned.1.call-start = ((), (), s32[]{:S(2)}) async-start(), calls=%async_computation.18 | async-start | bytes 5242880 | tf_op jit(solution)/shard_map/reduce_scatter | solution.py:198
  372.4 191.4 %reduce-scatter.17.cloned.1.call-start = ((), (), s32[]{:S(2)}) async-start(), calls=%async_computation.19 | async-start | bytes 5242880 | tf_op jit(solution)/shard_map/reduce_scatter | solution.py:201
  378.6 232.0 %reduce-scatter.11.cloned.1.call-start = ((), (), s32[]{:S(2)}) async-start(), calls=%async_computation.16 | async-start | bytes 3932160 | tf_op jit(solution)/shard_map/reduce_scatter | solution.py:192
  427.2 205.8 %all-reduce.14.cloned.1.call-start = ((), (), s32[]{:S(2)}) async-start(), calls=%async_computation.21 | async-start | bytes 2097152 | tf_op jit(solution)/shard_map/psum | solution.py:106
  435.6 324.0 %all-reduce.12.cloned.1.call-start = ((), (), s32[]{:S(2)}) async-start(), calls=%async_computation.20 | async-start | bytes 6291456 | tf_op jit(solution)/shard_map/psum | solution.py:206
  610.6 107.6 %copy-start.32 = (f32[1024]{0:T(1024)S(1)}, f32[1024]{0:T(1024)}, u32[]{:S(2)}) copy-start(f32[1024]{0:T(1024)} %param.27) | copy-start | bytes 12292
  632.9 85.3 %copy-start.8 = (bf16[256,1024]{1,0:T(8,128)(2,1)S(1)}, bf16[256,1024]{1,0:T(8,128)(2,1)}, u32[]{:S(2)}) copy-start(bf16[256,1024]{1,0:T(8,128)(2,1)} %get-tuple-element.230) | copy-start | bytes 1572868
  632.9 85.3 %copy-start.24 = (bf16[256,1024]{1,0:T(8,128)(2,1)S(1)}, bf16[256,1024]{1,0:T(8,128)(2,1)}, u32[]{:S(2)}) copy-start(bf16[256,1024]{1,0:T(8,128)(2,1)} %get-tuple-element.229) | copy-start | bytes 1572868
  (37 other events, 316.6 us)
Sparse Core Ops, SparseCore 0:
  9.8 46.5 all-gather.6
  59.2 27.9 all-gather.10
  89.4 27.3 all-gather.8
  118.4 25.7 all-gather.12
  147.0 18.5 all-reduce.7
  167.3 53.7 all-gather.14
  222.9 52.4 all-gather.16
  286.3 18.5 all-reduce.9
  366.3 28.4 reduce-scatter.8
  397.5 25.7 reduce-scatter.6
  426.3 26.4 reduce-scatter.12
  455.6 52.5 reduce-scatter.14
  511.2 52.5 reduce-scatter.16
  566.6 43.9 reduce-scatter.10
  613.4 19.4 all-reduce.13
  635.4 124.1 all-reduce.11
where the time goes:
time: 774 us; the launch traced here: 773 us
  waiting for transfers between devices  526 us (68%)
  matrix products  82.7 us (11%)
  blocking collectives  82.1 us (11%)
  local copies, waits for them, and re-layouts  30.8 us (4%)
  other arithmetic  27.4 us (4%)
  between operations  14.4 us (2%)
  loops' own time  8.03 us (1%)
    psum x1, blocking collectives, on_device(): lax.psum((g_bqv, g_bout, g_bfc, g_bproj, g_ln1g, g_ln1b, g_ln2g, g_ln2b),...  82.1 us
    reduce_scatter x1, waiting for transfers between devices, on_device(): lax.psum_scatter(g_proj.astype(jnp.bfloat16), 'shard', scatter_dimension=...  55.6 us
    reduce_scatter x1, waiting for transfers between devices, on_device(): lax.psum_scatter(g_fc.astype(jnp.bfloat16), 'shard', scatter_dimension=0,...  55.4 us
    all_gather x1, waiting for transfers between devices, on_device(): lax.all_gather(w_fc, 'shard', axis=0, tiled=True)  52.8 us
    all_gather x1, waiting for transfers between devices, on_device(): lax.all_gather(w_proj, 'shard', axis=1, tiled=True)  49.4 us
    dot_general x18, matrix products, dot32(): return jnp.dot(left, right, preferred_element_type=jnp.float32)  47.6 us
    reduce_scatter x1, waiting for transfers between devices, on_device(): lax.psum_scatter(g_qkv.astype(jnp.bfloat16), 'shard', scatter_dimension=1...  46.8 us
    all_gather x1, waiting for transfers between devices, on_device(): lax.all_gather(w_qkv, 'shard', axis=1, tiled=True)  45.1 us
  transfers between devices with their start and end apart: 16, of which 16 were waited for; matrix products, arithmetic and copies ran while one was open for 8% of the time, Pallas kernels for 0%

commit v1 on v0

--- a/solution.py
+++ b/solution.py
@@ -31,7 +31,7 @@
     return jnp.dot(left, right, preferred_element_type=jnp.float32)
 
 
-def on_device(
+def on_device_general(
     inputs,
     lengths,
     cotangent,
@@ -229,6 +229,247 @@
     )
 
 
+def exchange(pieces_of, place, count, axis):
+    me = lax.axis_index(axis)
+    arrived = [(me, pieces_of(me))]
+    for step in range(1, count):
+        pairs = [(i, i ^ step) for i in range(count)]
+        arrived.append((me ^ step, lax.ppermute(pieces_of(me ^ step), axis, pairs)))
+    return place(arrived)
+
+
+def all_to_all(values, count, split, concat):
+    width = values.shape[split] // count
+    depth = values.shape[concat]
+
+    def pieces_of(index):
+        return lax.dynamic_slice_in_dim(values, index * width, width, axis=split)
+
+    def place(arrived):
+        shape = list(values.shape)
+        shape[split] = width
+        shape[concat] = depth * count
+        result = jnp.zeros(shape, values.dtype)
+        for index, piece in arrived:
+            result = lax.dynamic_update_slice_in_dim(result, piece, index * depth, axis=concat)
+        return result
+
+    return exchange(pieces_of, place, count, "shard")
+
+
+def plane_gather(values):
+    return lax.all_gather(values, ("shard", "tp"), axis=0, tiled=True)
+
+
+def plane_scatter(values):
+    return lax.psum_scatter(
+        values.astype(jnp.bfloat16), ("shard", "tp"), scatter_dimension=0, tiled=True
+    ).astype(jnp.float32)
+
+
+def swap_planes(values, count):
+    pairs = [(a * count + b, b * count + a) for a in range(count) for b in range(count)]
+    return lax.ppermute(values, ("shard", "ctx"), pairs)
+
+
+def norm_back(values, gain, d_out):
+    mean = jnp.mean(values, axis=-1, keepdims=True)
+    centred = values - mean
+    scale = lax.rsqrt(jnp.mean(centred * centred, axis=-1, keepdims=True) + 1e-05)
+    unit = centred * scale
+    d_unit = d_out * gain
+    first = jnp.mean(d_unit, axis=-1, keepdims=True)
+    second = jnp.mean(d_unit * unit, axis=-1, keepdims=True)
+    d_values = (d_unit - first - unit * second) * scale
+    return d_values, jnp.sum(d_out * unit, axis=0), jnp.sum(d_out, axis=0)
+
+
+def attention(query, key, value, allowed, heads):
+    f32 = jnp.float32
+    parts = []
+    saved = []
+    for head in range(heads):
+        cols = slice(head * HEAD_DIM, (head + 1) * HEAD_DIM)
+        scores = lax.dot_general(
+            query[:, cols], key[:, cols], (((1,), (1,)), ((), ())), preferred_element_type=f32
+        )
+        weights = jnp.where(allowed, jnp.exp(scores), 0.0)
+        total = jnp.sum(weights, axis=1, keepdims=True)
+        parts.append(dot32(weights.astype(jnp.bfloat16), value[:, cols]) / total)
+        saved.append(jnp.log(total))
+    return jnp.concatenate(parts, axis=1).astype(jnp.bfloat16), saved
+
+
+def attention_back(query, key, value, attended, d_attended, allowed, saved, heads):
+    f32 = jnp.float32
+    bf = jnp.bfloat16
+    d_q, d_k, d_v = [], [], []
+    for head in range(heads):
+        cols = slice(head * HEAD_DIM, (head + 1) * HEAD_DIM)
+        q, k, v, da = query[:, cols], key[:, cols], value[:, cols], d_attended[:, cols]
+        delta = jnp.sum(da.astype(f32) * attended[:, cols].astype(f32), axis=1, keepdims=True)
+        scores = lax.dot_general(q, k, (((1,), (1,)), ((), ())), preferred_element_type=f32)
+        probs = jnp.where(allowed, jnp.exp(scores - saved[head]), 0.0)
+        d_v.append(
+            lax.dot_general(
+                probs.astype(bf), da, (((0,), (0,)), ((), ())), preferred_element_type=f32
+            )
+        )
+        d_probs = lax.dot_general(da, v, (((1,), (1,)), ((), ())), preferred_element_type=f32)
+        d_scores = (probs * (d_probs - delta)).astype(bf)
+        d_q.append(dot32(d_scores, k))
+        d_k.append(
+            lax.dot_general(d_scores, q, (((0,), (0,)), ((), ())), preferred_element_type=f32)
+        )
+    join = lambda items: jnp.concatenate(items, axis=1)
+    return join(d_q) * 0.125, join(d_k), join(d_v)
+
+
+def t_dot(left, right):
+    return lax.dot_general(left, right, (((0,), (0,)), ((), ())), preferred_element_type=jnp.float32)
+
+
+def dot_t(left, right):
+    return lax.dot_general(left, right, (((1,), (1,)), ((), ())), preferred_element_type=jnp.float32)
+
+
+def on_device_plane(
+    inputs,
+    lengths,
+    cotangent,
+    w_qkv,
+    w_out,
+    w_fc,
+    w_proj,
+    b_qv,
+    b_out,
+    b_fc,
+    b_proj,
+    ln1_gain,
+    ln1_bias,
+    ln2_gain,
+    ln2_bias,
+):
+    bf = jnp.bfloat16
+    f32 = jnp.float32
+    shards = lax.axis_size("shard")
+    cores = lax.axis_size("tp")
+    s = lax.axis_index("shard")
+    t = lax.axis_index("tp")
+    rows = inputs.shape[0] // cores
+    block = rows * cores * shards
+    model = inputs.shape[1]
+    width = b_qv.shape[1] // shards
+    heads = width // HEAD_DIM
+    units = b_fc.shape[0] // shards
+    mine = lambda array: lax.dynamic_slice_in_dim(array, t * rows, rows, axis=0)
+
+    x_f = swap_planes(mine(inputs), shards).astype(f32)
+    lens = swap_planes(lengths, shards)[0]
+    cot_own = swap_planes(mine(cotangent), shards)
+    normed1 = plane_gather(layer_norm(x_f, ln1_gain, ln1_bias).astype(bf))
+    wqkv = all_to_all(w_qkv, shards, 2, 1)
+    wout = all_to_all(w_out, shards, 0, 1)
+    wfc = all_to_all(w_fc, shards, 1, 0)
+    wproj = all_to_all(w_proj, shards, 0, 1)
+    cot = plane_gather(cot_own)
+    b_qv_own = lax.dynamic_slice_in_dim(b_qv, s * width, width, axis=1)
+    b_fc_own = lax.dynamic_slice_in_dim(b_fc, s * units, units, axis=0)
+
+    seg = segment_ids(lens, block)
+    places = jnp.arange(block, dtype=jnp.int32)
+    allowed = (places[None, :] <= places[:, None]) & (seg[None, :] == seg[:, None])
+
+    query = ((dot32(normed1, wqkv[0]) + b_qv_own[0]) * 0.125).astype(bf)
+    key = dot32(normed1, wqkv[1]).astype(bf)
+    value = (dot32(normed1, wqkv[2]) + b_qv_own[1]).astype(bf)
+    attended, saved = attention(query, key, value, allowed, heads)
+    hidden = x_f + plane_scatter(dot32(attended, wout)) + b_out
+    normed2 = plane_gather(layer_norm(hidden, ln2_gain, ln2_bias).astype(bf))
+    pre = dot32(normed2, wfc) + b_fc_own
+    act = gelu_tanh(pre).astype(bf)
+    d_act = dot_t(cot, wproj)
+    d_pre = jax.vjp(gelu_tanh, pre)[1](d_act)[0]
+    d_pre_b = d_pre.astype(bf)
+    d_normed2 = plane_scatter(dot_t(d_pre_b, wfc))
+    mlp_total = plane_scatter(dot32(act, wproj))
+    outputs = (hidden + mlp_total + b_proj).astype(bf)
+    g_proj = t_dot(act, cot)
+    g_fc = t_dot(normed2, d_pre_b)
+    g_bfc = jnp.sum(d_pre, axis=0)
+
+    cot_f = cot_own.astype(f32)
+    d_norm2, g_ln2g, g_ln2b = norm_back(hidden, ln2_gain, d_normed2)
+    d_hidden = cot_f + d_norm2
+    d_hidden_b = plane_gather(d_hidden.astype(bf))
+    g_out = t_dot(attended, d_hidden_b)
+    d_attended = dot_t(d_hidden_b, wout).astype(bf)
+    d_query, d_key, d_value = attention_back(
+        query, key, value, attended, d_attended, allowed, saved, heads
+    )
+    d_query_b, d_key_b, d_value_b = d_query.astype(bf), d_key.astype(bf), d_value.astype(bf)
+    d_normed1 = plane_scatter(
+        dot_t(d_query_b, wqkv[0]) + dot_t(d_key_b, wqkv[1]) + dot_t(d_value_b, wqkv[2])
+    )
+    g_qkv = jnp.stack([t_dot(normed1, d_query_b), t_dot(normed1, d_key_b), t_dot(normed1, d_value_b)])
+    d_norm1, g_ln1g, g_ln1b = norm_back(x_f, ln1_gain, d_normed1)
+    grad_inputs = (d_hidden + d_norm1).astype(bf)
+
+    def home(values):
+        return lax.all_gather(swap_planes(values, shards), "tp", axis=0, tiled=True)
+
+    def owner(grad, split, concat):
+        moved = all_to_all(grad.astype(bf), shards, split, concat)
+        return lax.psum(moved, "ctx").astype(f32)
+
+    sum_proj = owner(g_proj, 1, 0)
+    sum_fc = owner(g_fc, 0, 1)
+    sum_out = owner(g_out, 1, 0)
+    sum_qkv = owner(g_qkv, 1, 2)
+    col = t * b_qv.shape[1] + s * width
+    g_bqv = jnp.stack([jnp.sum(d_query, axis=0), jnp.sum(d_value, axis=0)])
+    full_bqv = lax.dynamic_update_slice(jnp.zeros((2, b_qv.shape[1] * cores), f32), g_bqv, (0, col))
+    full_bfc = lax.dynamic_update_slice(
+        jnp.zeros((b_fc.shape[0] * cores,), f32), g_bfc, (t * b_fc.shape[0] + s * units,)
+    )
+    packed = jnp.concatenate(
+        [
+            full_bqv.reshape(-1),
+            full_bfc,
+            jnp.sum(d_hidden, axis=0),
+            jnp.sum(cot_f, axis=0),
+            g_ln1g,
+            g_ln1b,
+            g_ln2g,
+            g_ln2b,
+        ]
+    )
+    packed = lax.psum(packed, ("shard", "ctx", "tp"))
+    at = full_bqv.size
+    sum_bqv = lax.dynamic_slice_in_dim(
+        packed[:at].reshape(full_bqv.shape), t * b_qv.shape[1], b_qv.shape[1], axis=1
+    )
+    sum_bfc = lax.dynamic_slice_in_dim(packed, at + t * b_fc.shape[0], b_fc.shape[0])
+    at = at + full_bfc.size
+    rest = packed[at:].reshape(6, model)
+    return (
+        home(outputs),
+        home(grad_inputs),
+        sum_qkv,
+        sum_out,
+        sum_fc,
+        sum_proj,
+        sum_bqv,
+        rest[0],
+        sum_bfc,
+        rest[1],
+        rest[2],
+        rest[3],
+        rest[4],
+        rest[5],
+    )
+
+
 def solution(mesh):
     in_specs = (
         P(("shard", "ctx"), None),
@@ -263,6 +504,9 @@
         P(),
         P(),
     )
+    count = mesh.shape["shard"]
+    square = count == mesh.shape["ctx"] and count & (count - 1) == 0
+    body = on_device_plane if square else on_device_general
     return jax.shard_map(
-        on_device, mesh=mesh, in_specs=in_specs, out_specs=out_specs, check_vma=False
-    )
+        body, mesh=mesh, in_specs=in_specs, out_specs=out_specs, check_vma=False
+    )

time: 774 us -> 575 us (0.74)
  waiting for transfers between devices: 526 us -> 312 us
  starting transfers between devices: 1.05 us -> 76.4 us
  matrix products: 82.7 us -> 54.9 us
  blocking collectives: 82.1 us -> 59.4 us
  loops' own time: 8.03 us -> 0 us
    all_gather x6 -> x4, waiting for transfers between devices: 220 us -> 53.7 us  [plane_gather(): return lax.all_gather(values, ('shard', 'tp'), axis=0, tiled=True)]
    reduce_scatter x6 -> x4, waiting for transfers between devices: 214 us -> 129 us  [plane_scatter(): lax.psum_scatter(values.astype(jnp.bfloat16), ('shard', 'tp'), scatter_di...]
    ppermute x0 -> x29, starting transfers between devices: none -> 75.3 us  [the longest x24 71.2 us: exchange(): arrived.append((me ^ step, lax.ppermute(pieces_of(me ^ step), axis, pairs)))]
    ppermute x0 -> x29, waiting for transfers between devices: none -> 43.3 us  [the longest x24 43.3 us: exchange(): arrived.append((me ^ step, lax.ppermute(pieces_of(me ^ step), axis, pairs)))]
    dot_general x18 -> x10, matrix products: 47.6 us -> 18 us  [dot32(): return jnp.dot(left, right, preferred_element_type=jnp.float32)]
    psum x1, blocking collectives: 82.1 us -> 55 us  [on_device_plane(): packed = lax.psum(packed, ('shard', 'ctx', 'tp'))]
    another operation x1 -> x0, loops' own time: 8.03 us -> none  [on_device(): lax.scan(back_piece, zero_query, (key_blocks, value_blocks, starts))]
    psum x4 -> x1, waiting for transfers between devices: 88.5 us -> 86.5 us  [owner(): return lax.psum(moved, 'ctx').astype(f32)]
  transfers between devices with their start and end apart: 16 -> 38, of which waited for: 16 -> 16; matrix products, arithmetic and copies ran while one was open for 8% -> 13% of each run, Pallas kernels for 0% -> 0%
where the time goes in v1:
time: 575 us; the launch traced here: 573 us
  waiting for transfers between devices  312 us (54%)
  starting transfers between devices  76.4 us (13%)
  blocking collectives  59.4 us (10%)
  matrix products  54.9 us (10%)
  local copies, waits for them, and re-layouts  33.5 us (6%)
  other arithmetic  22.1 us (4%)
  between operations  15.2 us (3%)
    reduce_scatter x4, waiting for transfers between devices, plane_scatter(): lax.psum_scatter(values.astype(jnp.bfloat16), ('shard', 'tp'), scatter_di...  129 us
    psum x1, waiting for transfers between devices, owner(): return lax.psum(moved, 'ctx').astype(f32)  86.5 us
    ppermute x24, starting transfers between devices, exchange(): arrived.append((me ^ step, lax.ppermute(pieces_of(me ^ step), axis, pairs)))  71.2 us
    psum x1, blocking collectives, on_device_plane(): packed = lax.psum(packed, ('shard', 'ctx', 'tp'))  55 us
    all_gather x4, waiting for transfers between devices, plane_gather(): return lax.all_gather(values, ('shard', 'tp'), axis=0, tiled=True)  53.7 us
    ppermute x24, waiting for transfers between devices, exchange(): arrived.append((me ^ step, lax.ppermute(pieces_of(me ^ step), axis, pairs)))  43.3 us
    dot_general x10, matrix products, dot32(): return jnp.dot(left, right, preferred_element_type=jnp.float32)  18 us
    dot_general x6, matrix products, dot_t(): lax.dot_general(left, right, (((1,), (1,)), ((), ())), preferred_element_...  15.8 us
  transfers between devices with their start and end apart: 38, of which 16 were waited for; matrix products, arithmetic and copies ran while one was open for 13% of the time, Pallas kernels for 0%

profile of v1, /device:TPU:0, one launch (start us, length us, event | category | flops | bytes accessed | tf_op | source)
XLA Modules:
  0.0 573.5 jit_solution(12057198484178978346)
XLA Ops:
  12.4 21.2 %collective-permute-start.7 = (bf16[128,256]{1,0:T(8,128)(2,1)S(1)}, bf16[128,256]{1,0:T(8,128)(2,1)S(1)}, u32[]{:S(2)}, u32[]{:S(2)}) collective-permute-start(bf16[128,256]{1,0:T(8,128)(2,1)S(1)} %get-tuple-element.64), channel_id=1, source_target_pairs={{0,24},{8,16},{16,8},{24,0},{1,25},{9,17},{17,9},{25,1},{2,26},{10... | collective-permute-start | bytes 196616 | tf_op jit(solution)/shard_map/ppermute | solution.py:237
  33.6 4.0 collective-permute-start.5
  44.0 7.7 %collective-permute-done.2 = bf16[3,256,128]{2,1,0:T(8,128)(2,1)S(1)} collective-permute-done((bf16[3,256,128]{2,1,0:T(8,128)(2,1)S(1)}, bf16[3,256,128]{2,1,0:T(8,128)(2,1)S(1)}, u32[]{:S(2)}, u32[]{:S(2)}) %collective-permute-start.2) | collective-permute-done | bytes 196640 | tf_op jit(solution)/shard_map/ppermute | solution.py:237
  53.2 14.3 %all-gather.5.cloned.1.call-done = bf16[1024,1024]{1,0:T(8,128)(2,1)} async-done(((bf16[128,1024]{1,0:T(8,128)(2,1)}), bf16[1024,1024]{1,0:T(8,128)(2,1)}) %all-gather.5.cloned.1.call-update) | async-done | bytes 2097168 | tf_op jit(solution)/shard_map/all_gather | solution.py:261
  78.7 41.2 %reduce-scatter.5.cloned.1.call-done = bf16[128,1024]{1,0:T(8,128)(2,1)} async-done(((bf16[1024,1024]{1,0:T(8,128)(2,1)}), bf16[128,1024]{1,0:T(8,128)(2,1)}) %reduce-scatter.5.cloned.1.call-update) | async-done | bytes 262160 | tf_op jit(solution)/shard_map/reduce_scatter | solution.py:265
  129.9 22.7 %collective-permute-start.11 = (bf16[512,256]{1,0:T(8,128)(2,1)S(1)}, bf16[512,256]{1,0:T(8,128)(2,1)S(1)}, u32[]{:S(2)}, u32[]{:S(2)}) collective-permute-start(bf16[512,256]{1,0:T(8,128)(2,1)S(1)} %get-tuple-element.47), channel_id=1, source_target_pairs={{0,8},{8,0},{16,24},{24,16},{1,9},{9,1},{17,25},{25,17},{2,10},{10... | collective-permute-start | bytes 786440 | tf_op jit(solution)/shard_map/ppermute | solution.py:237
  158.8 3.9 collective-permute-done.11
  163.4 10.5 %collective-permute-done.12 = bf16[512,256]{1,0:T(8,128)(2,1)S(1)} collective-permute-done((bf16[512,256]{1,0:T(8,128)(2,1)S(1)}, bf16[512,256]{1,0:T(8,128)(2,1)S(1)}, u32[]{:S(2)}, u32[]{:S(2)}) %collective-permute-start.12) | collective-permute-done | bytes 262176 | tf_op jit(solution)/shard_map/ppermute | solution.py:237
  175.4 3.6 collective-permute-done.8
  181.2 4.5 fusion.121
  185.7 16.8 %all-gather.9.cloned.1.call-done = bf16[1024,1024]{1,0:T(8,128)(2,1)} async-done(((bf16[128,1024]{1,0:T(8,128)(2,1)}), bf16[1024,1024]{1,0:T(8,128)(2,1)}) %all-gather.9.cloned.1.call-update) | async-done | bytes 2097168 | tf_op jit(solution)/shard_map/all_gather | solution.py:261
  202.5 6.0 %fusion.117 = (f32[512]{0:T(512)}, bf16[1024,512]{1,0:T(8,128)(2,1)S(1)}) fusion(f32[1024,512]{1,0:T(8,128)} %fusion.121, f32[512]{0:T(512)S(1)} %dynamic_slice.128, bf16[1024,1024]{1,0:T(8,128)(2,1)} %all-gather.9.cloned.1.call-done, bf16[512,1024]{1,0:T(8,128)(2,1)} %constant_dynamic-update-slice_fusion.13), kind=kOutput, calls=%fused_computation.231 | convolution fusion | flops 1087372800 | bytes 6295552 | tf_op jit(solution)/shard_map/dot_general | solution.py:333
  209.5 3.8 convolution_convert_fusion
  213.4 4.8 convolution_convert_fusion.1
  218.2 36.3 %reduce-scatter.9.cloned.1.call-done = bf16[128,1024]{1,0:T(8,128)(2,1)} async-done(((bf16[1024,1024]{1,0:T(8,128)(2,1)}), bf16[128,1024]{1,0:T(8,128)(2,1)}) %reduce-scatter.9.cloned.1.call-update) | async-done | bytes 262160 | tf_op jit(solution)/shard_map/reduce_scatter | solution.py:265
  256.4 42.5 %reduce-scatter.7.cloned.1.call-done = bf16[128,1024]{1,0:T(8,128)(2,1)} async-done(((bf16[1024,1024]{1,0:T(8,128)(2,1)}), bf16[128,1024]{1,0:T(8,128)(2,1)}) %reduce-scatter.7.cloned.1.call-update) | async-done | bytes 262160 | tf_op jit(solution)/shard_map/reduce_scatter | solution.py:265
  306.1 3.6 convolution_convert_fusion.3
  315.3 22.6 %all-gather.11.cloned.1.call-done = bf16[1024,1024]{1,0:T(8,128)(2,1)} async-done(((bf16[128,1024]{1,0:T(8,128)(2,1)}), bf16[1024,1024]{1,0:T(8,128)(2,1)}) %all-gather.11.cloned.1.call-update) | async-done | bytes 2097168 | tf_op jit(solution)/shard_map/all_gather | solution.py:261
  340.5 3.1 fusion.20
  368.4 6.4 %collective-permute-done.23 = bf16[256,512]{1,0:T(8,128)(2,1)S(1)} collective-permute-done((bf16[256,512]{1,0:T(8,128)(2,1)S(1)}, bf16[256,512]{1,0:T(8,128)(2,1)S(1)}, u32[]{:S(2)}, u32[]{:S(2)}) %collective-permute-start.23) | collective-permute-done | bytes 262176 | tf_op jit(solution)/shard_map/ppermute | solution.py:237
  386.1 9.7 %collective-permute-done.17 = bf16[3,256,128]{2,1,0:T(8,128)(2,1)S(1)} collective-permute-done((bf16[3,256,128]{2,1,0:T(8,128)(2,1)S(1)}, bf16[3,256,128]{2,1,0:T(8,128)(2,1)S(1)}, u32[]{:S(2)}, u32[]{:S(2)}) %collective-permute-start.17) | collective-permute-done | bytes 196640 | tf_op jit(solution)/shard_map/ppermute | solution.py:237
  400.6 8.6 %reduce-scatter.11.cloned.1.call-done = bf16[128,1024]{1,0:T(8,128)(2,1)} async-done(((bf16[1024,1024]{1,0:T(8,128)(2,1)}), bf16[128,1024]{1,0:T(8,128)(2,1)}) %reduce-scatter.11.cloned.1.call-update) | async-done | bytes 262160 | tf_op jit(solution)/shard_map/reduce_scatter | solution.py:265
  410.5 55.0 %psum.39 = f32[12288]{0:T(1024)S(1)} all-reduce(f32[12288]{0:T(1024)S(1)} %constant_dynamic-update-slice_fusion.25), channel_id=1, replica_groups=mesh['shard'=4,'ctx'=4,'tp'=2] {'shard','ctx','tp'}, use_global_device_ids=true, to_apply=%region_31.32 | all-reduce | flops 12288 | bytes 98304 | tf_op jit(solution)/shard_map/psum | solution.py:447
  469.3 86.5 %all-reduce.3.cloned.1.call-done = (bf16[3,256,512]{2,1,0:T(8,128)(2,1)}, bf16[512,256]{1,0:T(8,128)(2,1)}, bf16[256,2048]{1,0:T(8,128)(2,1)}, bf16[2048,256]{1,0:T(8,128)(2,1)}) async-done(((bf16[3,256,512]{2,1,0:T(8,128)(2,1)}, bf16[512,256]{1,0:T(8,128)(2,1)}, bf16[256,2048]{1,0:T(8,128)(2,1)}, bf16[2048,256]{1,0:T(8,128)(2,1)}), (bf16[3,256,512]{2,1,0:T(8,128)(2,1)}, bf16[512,256]{1,0:T(8,128)(2,1)}, ...) | async-done | bytes 3145744 | tf_op jit(solution)/shard_map/psum | solution.py:423
  (313 shorter events, 118.9 us)
Async XLA Ops:
  7.2 60.3 %all-gather.5.cloned.1.call-start = ((), (), s32[]{:S(2)}) async-start(), calls=%async_computation.4 | async-start | bytes 2359296 | tf_op jit(solution)/shard_map/all_gather | solution.py:261
  11.0 108.9 %reduce-scatter.5.cloned.1.call-start = ((), (), s32[]{:S(2)}) async-start(), calls=%async_computation.5 | async-start | bytes 2359296 | tf_op jit(solution)/shard_map/reduce_scatter | solution.py:265
  11.0 30.4 %collective-permute-start.1 = (s32[1,3]{1,0:T(1,128)}, s32[1,3]{1,0:T(1,128)S(1)}, u32[]{:S(2)}, u32[]{:S(2)}) collective-permute-start(s32[1,3]{1,0:T(1,128)} %param.16), channel_id=1, source_target_pairs={{0,0},{2,8},{4,16},{6,24},{8,2},{10,10},{12,18},{14,26},{16,4},{18... | collective-permute-start | bytes 44 | tf_op jit(solution)/shard_map/ppermute | solution.py:272
  12.4 31.5 %collective-permute-start.7 = (bf16[128,256]{1,0:T(8,128)(2,1)S(1)}, bf16[128,256]{1,0:T(8,128)(2,1)S(1)}, u32[]{:S(2)}, u32[]{:S(2)}) collective-permute-start(bf16[128,256]{1,0:T(8,128)(2,1)S(1)} %get-tuple-element.64), channel_id=1, source_target_pairs={{0,24},{8,16},{16,8},{24,0},{1,25},{9,17},{17,9},{25,1},{2,26},{10... | collective-permute-start | bytes 196616 | tf_op jit(solution)/shard_map/ppermute | solution.py:237
  39.3 13.9 %collective-permute-start.4 = (bf16[3,256,128]{2,1,0:T(8,128)(2,1)S(1)}, bf16[3,256,128]{2,1,0:T(8,128)(2,1)S(1)}, u32[]{:S(2)}, u32[]{:S(2)}) collective-permute-start(bf16[3,256,128]{2,1,0:T(8,128)(2,1)S(1)} %get-tuple-element.54), channel_id=1, source_target_pairs={{0,24},{8,16},{16,8},{24,0},{1,25},{9,17},{17,9},{25,1},{2,26},{10... | collective-permute-start | bytes 589832 | tf_op jit(solution)/shard_map/ppermute | solution.py:237
  78.6 102.6 %all-gather.7.cloned.1.call-start = ((), (), s32[]{:S(2)}) async-start(), calls=%async_computation.6 | async-start | bytes 2359296 | tf_op jit(solution)/shard_map/all_gather | solution.py:261
  124.1 78.4 %all-gather.9.cloned.1.call-start = ((), (), s32[]{:S(2)}) async-start(), calls=%async_computation.8 | async-start | bytes 2359296 | tf_op jit(solution)/shard_map/all_gather | solution.py:261
  126.5 128.0 %reduce-scatter.9.cloned.1.call-start = ((), (), s32[]{:S(2)}) async-start(), calls=%async_computation.9 | async-start | bytes 2359296 | tf_op jit(solution)/shard_map/reduce_scatter | solution.py:265
  129.9 32.7 %collective-permute-start.11 = (bf16[512,256]{1,0:T(8,128)(2,1)S(1)}, bf16[512,256]{1,0:T(8,128)(2,1)S(1)}, u32[]{:S(2)}, u32[]{:S(2)}) collective-permute-start(bf16[512,256]{1,0:T(8,128)(2,1)S(1)} %get-tuple-element.47), channel_id=1, source_target_pairs={{0,8},{8,0},{16,24},{24,16},{1,9},{9,1},{17,25},{25,17},{2,10},{10... | collective-permute-start | bytes 786440 | tf_op jit(solution)/shard_map/ppermute | solution.py:237
  152.7 21.3 %collective-permute-start.12 = (bf16[512,256]{1,0:T(8,128)(2,1)S(1)}, bf16[512,256]{1,0:T(8,128)(2,1)S(1)}, u32[]{:S(2)}, u32[]{:S(2)}) collective-permute-start(bf16[512,256]{1,0:T(8,128)(2,1)S(1)} %get-tuple-element.49), channel_id=1, source_target_pairs={{0,16},{8,24},{16,0},{24,8},{1,17},{9,25},{17,1},{25,9},{2,18},{10... | collective-permute-start | bytes 786440 | tf_op jit(solution)/shard_map/ppermute | solution.py:237
  152.7 22.0 %collective-permute-start.13 = (bf16[512,256]{1,0:T(8,128)(2,1)S(1)}, bf16[512,256]{1,0:T(8,128)(2,1)S(1)}, u32[]{:S(2)}, u32[]{:S(2)}) collective-permute-start(bf16[512,256]{1,0:T(8,128)(2,1)S(1)} %get-tuple-element.46), channel_id=1, source_target_pairs={{0,24},{8,16},{16,8},{24,0},{1,25},{9,17},{17,9},{25,1},{2,26},{10... | collective-permute-start | bytes 786440 | tf_op jit(solution)/shard_map/ppermute | solution.py:237
  156.0 24.5 %collective-permute-start.10 = (bf16[256,512]{1,0:T(8,128)(2,1)S(1)}, bf16[256,512]{1,0:T(8,128)(2,1)S(1)}, u32[]{:S(2)}, u32[]{:S(2)}) collective-permute-start(bf16[256,512]{1,0:T(8,128)(2,1)S(1)} %get-tuple-element.42), channel_id=1, source_target_pairs={{0,24},{8,16},{16,8},{24,0},{1,25},{9,17},{17,9},{25,1},{2,26},{10... | collective-permute-start | bytes 786440 | tf_op jit(solution)/shard_map/ppermute | solution.py:237
  157.4 21.6 %collective-permute-start.8 = (bf16[256,512]{1,0:T(8,128)(2,1)S(1)}, bf16[256,512]{1,0:T(8,128)(2,1)S(1)}, u32[]{:S(2)}, u32[]{:S(2)}) collective-permute-start(bf16[256,512]{1,0:T(8,128)(2,1)S(1)} %get-tuple-element.43), channel_id=1, source_target_pairs={{0,8},{8,0},{16,24},{24,16},{1,9},{9,1},{17,25},{25,17},{2,10},{10... | collective-permute-start | bytes 786440 | tf_op jit(solution)/shard_map/ppermute | solution.py:237
  162.6 17.1 %collective-permute-start.9 = (bf16[256,512]{1,0:T(8,128)(2,1)S(1)}, bf16[256,512]{1,0:T(8,128)(2,1)S(1)}, u32[]{:S(2)}, u32[]{:S(2)}) collective-permute-start(bf16[256,512]{1,0:T(8,128)(2,1)S(1)} %get-tuple-element.45), channel_id=1, source_target_pairs={{0,16},{8,24},{16,0},{24,8},{1,17},{9,25},{17,1},{25,9},{2,18},{10... | collective-permute-start | bytes 786440 | tf_op jit(solution)/shard_map/ppermute | solution.py:237
  213.3 85.5 %reduce-scatter.7.cloned.1.call-start = ((), (), s32[]{:S(2)}) async-start(), calls=%async_computation.7 | async-start | bytes 2359296 | tf_op jit(solution)/shard_map/reduce_scatter | solution.py:265
  218.2 119.7 %all-gather.11.cloned.1.call-start = ((), (), s32[]{:S(2)}) async-start(), calls=%async_computation.10 | async-start | bytes 2359296 | tf_op jit(solution)/shard_map/all_gather | solution.py:261
  303.3 106.0 %reduce-scatter.11.cloned.1.call-start = ((), (), s32[]{:S(2)}) async-start(), calls=%async_computation.11 | async-start | bytes 2359296 | tf_op jit(solution)/shard_map/reduce_scatter | solution.py:265
  311.8 54.9 %collective-permute-start.28 = (bf16[512,256]{1,0:T(8,128)(2,1)}, bf16[512,256]{1,0:T(8,128)(2,1)}, u32[]{:S(2)}, u32[]{:S(2)}) collective-permute-start(bf16[512,256]{1,0:T(8,128)(2,1)} %get-tuple-element.34), channel_id=1, source_target_pairs={{0,24},{8,16},{16,8},{24,0},{1,25},{9,17},{17,9},{25,1},{2,26},{10... | collective-permute-start | bytes 786440 | tf_op jit(solution)/shard_map/ppermute | solution.py:237
  313.3 51.7 %collective-permute-start.27 = (bf16[512,256]{1,0:T(8,128)(2,1)}, bf16[512,256]{1,0:T(8,128)(2,1)}, u32[]{:S(2)}, u32[]{:S(2)}) collective-permute-start(bf16[512,256]{1,0:T(8,128)(2,1)} %get-tuple-element.35), channel_id=1, source_target_pairs={{0,16},{8,24},{16,0},{24,8},{1,17},{9,25},{17,1},{25,9},{2,18},{10... | collective-permute-start | bytes 786440 | tf_op jit(solution)/shard_map/ppermute | solution.py:237
  314.7 48.0 %collective-permute-start.26 = (bf16[512,256]{1,0:T(8,128)(2,1)}, bf16[512,256]{1,0:T(8,128)(2,1)}, u32[]{:S(2)}, u32[]{:S(2)}) collective-permute-start(bf16[512,256]{1,0:T(8,128)(2,1)} %get-tuple-element.36), channel_id=1, source_target_pairs={{0,8},{8,0},{16,24},{24,16},{1,9},{9,1},{17,25},{25,17},{2,10},{10... | collective-permute-start | bytes 786440 | tf_op jit(solution)/shard_map/ppermute | solution.py:237
  356.0 199.7 %all-reduce.3.cloned.1.call-start = ((), (), s32[]{:S(2)}) async-start(), calls=%async_computation.12 | async-start | bytes 6291456 | tf_op jit(solution)/shard_map/psum | solution.py:423
  359.7 15.1 %collective-permute-start.25 = (bf16[256,512]{1,0:T(8,128)(2,1)S(1)}, bf16[256,512]{1,0:T(8,128)(2,1)S(1)}, u32[]{:S(2)}, u32[]{:S(2)}) collective-permute-start(bf16[256,512]{1,0:T(8,128)(2,1)S(1)} %get-tuple-element.38), channel_id=1, source_target_pairs={{0,24},{8,16},{16,8},{24,0},{1,25},{9,17},{17,9},{25,1},{2,26},{10... | collective-permute-start | bytes 786440 | tf_op jit(solution)/shard_map/ppermute | solution.py:237
  381.8 14.1 %collective-permute-start.19 = (bf16[3,256,128]{2,1,0:T(8,128)(2,1)S(1)}, bf16[3,256,128]{2,1,0:T(8,128)(2,1)S(1)}, u32[]{:S(2)}, u32[]{:S(2)}) collective-permute-start(bf16[3,256,128]{2,1,0:T(8,128)(2,1)S(1)} %get-tuple-element.50), channel_id=1, source_target_pairs={{0,24},{8,16},{16,8},{24,0},{1,25},{9,17},{17,9},{25,1},{2,26},{10... | collective-permute-start | bytes 589832 | tf_op jit(solution)/shard_map/ppermute | solution.py:237
  467.4 95.8 %collective-permute-start.16 = (bf16[128,1024]{1,0:T(8,128)(2,1)S(1)}, bf16[128,1024]{1,0:T(8,128)(2,1)S(1)}, u32[]{:S(2)}, u32[]{:S(2)}) collective-permute-start(bf16[128,1024]{1,0:T(8,128)(2,1)S(1)} %fusion.59), channel_id=1, source_target_pairs={{0,0},{2,8},{4,16},{6,24},{8,2},{10,10},{12,18},{14,26},{16,4},{18... | collective-permute-start | bytes 786440 | tf_op jit(solution)/shard_map/ppermute | solution.py:272
  (77 other events, 760.7 us)
Sparse Core Ops, SparseCore 0:
  11.1 56.3 all-gather.4
  78.8 41.0 reduce-scatter.4
  124.2 37.4 all-gather.6
  163.9 38.5 all-gather.8
  213.4 41.0 reduce-scatter.8
  257.7 41.1 reduce-scatter.6
  303.4 34.4 all-gather.10
  356.2 53.0 reduce-scatter.10
  412.4 143.3 all-reduce.2

commit v2 on v1

--- a/solution.py
+++ b/solution.py
@@ -1,6 +1,8 @@
 import jax
 import jax.numpy as jnp
 from jax import lax
+from jax.experimental import pallas as pl
+from jax.experimental.pallas import tpu as pltpu
 from jax.sharding import PartitionSpec as P
 
 HEAD_DIM = 64
@@ -229,42 +231,262 @@
     )
 
 
-def exchange(pieces_of, place, count, axis):
-    me = lax.axis_index(axis)
-    arrived = [(me, pieces_of(me))]
-    for step in range(1, count):
-        pairs = [(i, i ^ step) for i in range(count)]
-        arrived.append((me ^ step, lax.ppermute(pieces_of(me ^ step), axis, pairs)))
-    return place(arrived)
-
-
-def all_to_all(values, count, split, concat):
-    width = values.shape[split] // count
-    depth = values.shape[concat]
-
-    def pieces_of(index):
-        return lax.dynamic_slice_in_dim(values, index * width, width, axis=split)
-
-    def place(arrived):
-        shape = list(values.shape)
-        shape[split] = width
-        shape[concat] = depth * count
-        result = jnp.zeros(shape, values.dtype)
-        for index, piece in arrived:
-            result = lax.dynamic_update_slice_in_dim(result, piece, index * depth, axis=concat)
-        return result
-
-    return exchange(pieces_of, place, count, "shard")
+MESH = pl.DeviceIdType.MESH
+VMEM = pl.BlockSpec(memory_space=pltpu.VMEM)
+
+
+def greet(peers):
+    barrier = pltpu.get_barrier_semaphore()
+    for peer in peers:
+        pl.semaphore_signal(barrier, inc=1, device_id=peer, device_id_type=MESH)
+    pl.semaphore_wait(barrier, len(peers))
+
+
+def send(src, dst, send_sem, recv_sem, peer):
+    copy = pltpu.make_async_remote_copy(
+        src_ref=src,
+        dst_ref=dst,
+        send_sem=send_sem,
+        recv_sem=recv_sem,
+        device_id=peer,
+        device_id_type=MESH,
+    )
+    copy.start()
+    return copy
+
+
+def comm_call(kernel, out_shape, scratch, ident, cost, *operands):
+    many = isinstance(out_shape, (list, tuple))
+    return pl.pallas_call(
+        kernel,
+        out_shape=out_shape,
+        in_specs=[VMEM] * len(operands),
+        out_specs=[VMEM] * len(out_shape) if many else VMEM,
+        scratch_shapes=scratch,
+        compiler_params=pltpu.CompilerParams(collective_id=ident, has_side_effects=True),
+        cost_estimate=pl.CostEstimate(flops=0, bytes_accessed=cost, transcendentals=0),
+    )(*operands)
+
+
+def all_to_all(arrays, cuts, ident):
+    count = lax.axis_size("shard")
+    shapes = []
+    for array, (split, concat) in zip(arrays, cuts):
+        shape = list(array.shape)
+        shape[split] //= count
+        shape[concat] *= count
+        shapes.append(jax.ShapeDtypeStruct(tuple(shape), array.dtype))
+    total = len(arrays)
+
+    def kernel(*refs):
+        ins, outs = refs[:total], refs[total : 2 * total]
+        send_sem, recv_sem, own_sem = refs[2 * total :]
+        me = lax.axis_index("shard")
+        greet([{"shard": me ^ step} for step in range(1, count)])
+
+        def view(ref, axis, index, size):
+            start = pl.multiple_of(index * size, size)
+            return ref.at[tuple(pl.ds(start, size) if d == axis else slice(None) for d in range(len(ref.shape)))]
+
+        copies = []
+        for a, (split, concat) in enumerate(cuts):
+            width = ins[a].shape[split] // count
+            depth = ins[a].shape[concat]
+            for step in range(count - 1, 0, -1):
+                at = a * (count - 1) + step - 1
+                copies.append(
+                    send(
+                        view(ins[a], split, me ^ step, width),
+                        view(outs[a], concat, me, depth),
+                        send_sem.at[at],
+                        recv_sem.at[at],
+                        {"shard": me ^ step},
+                    )
+                )
+            own = pltpu.make_async_copy(
+                view(ins[a], split, me, width), view(outs[a], concat, me, depth), own_sem.at[a]
+            )
+            own.start()
+            copies.append(own)
+        for copy in copies:
+            copy.wait()
+
+    sems = total * (count - 1)
+    return comm_call(
+        kernel,
+        shapes,
+        [
+            pltpu.SemaphoreType.DMA((sems,)),
+            pltpu.SemaphoreType.DMA((sems,)),
+            pltpu.SemaphoreType.DMA((total,)),
+        ],
+        ident,
+        1 << 24,
+        *arrays,
+    )
 
 
 def plane_gather(values):
-    return lax.all_gather(values, ("shard", "tp"), axis=0, tiled=True)
+    count = lax.axis_size("shard")
+    rows, cols = values.shape
+
+    def kernel(x_ref, o_ref, send_sem, recv_sem, pass_sem, pair_sem, own_sem):
+        s, t = lax.axis_index("shard"), lax.axis_index("tp")
+        other = {"tp": 1 - t}
+        greet([other] + [{"shard": s ^ step} for step in range(1, count)])
+
+        def slot(index):
+            return o_ref.at[pl.ds(pl.multiple_of((index * 2 + t) * rows, rows), rows)]
+
+        own = pltpu.make_async_copy(x_ref, slot(s), own_sem)
+        own.start()
+        copies = {}
+        for step in range(count - 1, 0, -1):
+            copies[step] = send(
+                x_ref, slot(s), send_sem.at[step - 1], recv_sem.at[step - 1], {"shard": s ^ step}
+            )
+        passed = [send(x_ref, slot(s), pass_sem.at[0], pair_sem.at[0], other)]
+        for step in range(1, count):
+            copies[step].wait_recv()
+            passed.append(
+                send(slot(s ^ step), slot(s ^ step), pass_sem.at[step], pair_sem.at[step], other)
+            )
+        for copy in passed:
+            copy.wait()
+        for step in range(1, count):
+            copies[step].wait_send()
+        own.wait()
+
+    return comm_call(
+        kernel,
+        jax.ShapeDtypeStruct((rows * count * 2, cols), values.dtype),
+        [
+            pltpu.SemaphoreType.DMA((count - 1,)),
+            pltpu.SemaphoreType.DMA((count - 1,)),
+            pltpu.SemaphoreType.DMA((count,)),
+            pltpu.SemaphoreType.DMA((count,)),
+            pltpu.SemaphoreType.DMA,
+        ],
+        1,
+        1 << 24,
+        values,
+    )
 
 
 def plane_scatter(values):
-    return lax.psum_scatter(
-        values.astype(jnp.bfloat16), ("shard", "tp"), scatter_dimension=0, tiled=True
-    ).astype(jnp.float32)
+    count = lax.axis_size("shard")
+    rows, cols = values.shape[0] // (count * 2), values.shape[1]
+    f32 = jnp.float32
+    bf = jnp.bfloat16
+
+    def kernel(p_ref, o_ref, got, staged, arrived, pass_sem, pair_sem, send_sem, recv_sem):
+        s, t = lax.axis_index("shard"), lax.axis_index("tp")
+        other = {"tp": 1 - t}
+        greet([other] + [{"shard": s ^ step} for step in range(1, count)])
+
+        def chunk(index, core):
+            return p_ref.at[pl.ds(pl.multiple_of((index * 2 + core) * rows, rows), rows)]
+
+        order = list(range(count - 1, -1, -1))
+        first = {}
+        for step in order:
+            first[step] = send(
+                chunk(s ^ step, 1 - t), got.at[step], pass_sem.at[step], pair_sem.at[step], other
+            )
+        second = []
+        for step in order:
+            first[step].wait_recv()
+            total = chunk(s ^ step, t)[...].astype(f32) + got[step].astype(f32)
+            if step > 0:
+                staged[step - 1] = total.astype(bf)
+                second.append(
+                    send(
+                        staged.at[step - 1],
+                        arrived.at[step - 1],
+                        send_sem.at[step - 1],
+                        recv_sem.at[step - 1],
+                        {"shard": s ^ step},
+                    )
+                )
+            else:
+                o_ref[...] = total
+        for copy, step in zip(second, order):
+            copy.wait_recv()
+            o_ref[...] += arrived[step - 1].astype(f32)
+        for step in order:
+            first[step].wait_send()
+        for copy in second:
+            copy.wait_send()
+
+    return comm_call(
+        kernel,
+        jax.ShapeDtypeStruct((rows, cols), f32),
+        [
+            pltpu.VMEM((count, rows, cols), bf),
+            pltpu.VMEM((count - 1, rows, cols), bf),
+            pltpu.VMEM((count - 1, rows, cols), bf),
+            pltpu.SemaphoreType.DMA((count,)),
+            pltpu.SemaphoreType.DMA((count,)),
+            pltpu.SemaphoreType.DMA((count - 1,)),
+            pltpu.SemaphoreType.DMA((count - 1,)),
+        ],
+        2,
+        1 << 24,
+        values.astype(bf),
+    )
+
+
+def sum_everywhere(values):
+    shards, lines = lax.axis_size("shard"), lax.axis_size("ctx")
+    shape = values.shape
+
+    def kernel(x_ref, o_ref, got, staged, arrived, send_sem, recv_sem, line_send, line_recv):
+        s, c, t = lax.axis_index("shard"), lax.axis_index("ctx"), lax.axis_index("tp")
+        plane = [
+            {"shard": s ^ step, "tp": 1 - t if swap else t}
+            for step in range(shards)
+            for swap in range(2)
+            if step or swap
+        ]
+        line = [{"ctx": c ^ step} for step in range(1, lines)]
+        greet(plane + line)
+        copies = [
+            send(x_ref, got.at[i], send_sem.at[i], recv_sem.at[i], peer)
+            for i, peer in enumerate(plane)
+        ]
+        total = x_ref[...]
+        for i, copy in enumerate(copies):
+            copy.wait_recv()
+            total = total + got[i]
+        staged[...] = total
+        o_ref[...] = total
+        lines_out = [
+            send(staged, arrived.at[i], line_send.at[i], line_recv.at[i], peer)
+            for i, peer in enumerate(line)
+        ]
+        for i, copy in enumerate(lines_out):
+            copy.wait_recv()
+            o_ref[...] += arrived[i]
+        for copy in copies + lines_out:
+            copy.wait_send()
+
+    near, far = shards * 2 - 1, lines - 1
+    return comm_call(
+        kernel,
+        jax.ShapeDtypeStruct(shape, values.dtype),
+        [
+            pltpu.VMEM((near,) + shape, values.dtype),
+            pltpu.VMEM(shape, values.dtype),
+            pltpu.VMEM((far,) + shape, values.dtype),
+            pltpu.SemaphoreType.DMA((near,)),
+            pltpu.SemaphoreType.DMA((near,)),
+            pltpu.SemaphoreType.DMA((far,)),
+            pltpu.SemaphoreType.DMA((far,)),
+        ],
+        3,
+        1 << 22,
+        values,
+    )
 
 
 def swap_planes(values, count):
@@ -368,10 +590,9 @@
     lens = swap_planes(lengths, shards)[0]
     cot_own = swap_planes(mine(cotangent), shards)
     normed1 = plane_gather(layer_norm(x_f, ln1_gain, ln1_bias).astype(bf))
-    wqkv = all_to_all(w_qkv, shards, 2, 1)
-    wout = all_to_all(w_out, shards, 0, 1)
-    wfc = all_to_all(w_fc, shards, 1, 0)
-    wproj = all_to_all(w_proj, shards, 0, 1)
+    wqkv, wout, wfc, wproj = all_to_all(
+        [w_qkv, w_out, w_fc, w_proj], [(2, 1), (0, 1), (1, 0), (0, 1)], 4
+    )
     cot = plane_gather(cot_own)
     b_qv_own = lax.dynamic_slice_in_dim(b_qv, s * width, width, axis=1)
     b_fc_own = lax.dynamic_slice_in_dim(b_fc, s * units, units, axis=0)
@@ -418,14 +639,16 @@
     def home(values):
         return lax.all_gather(swap_planes(values, shards), "tp", axis=0, tiled=True)
 
-    def owner(grad, split, concat):
-        moved = all_to_all(grad.astype(bf), shards, split, concat)
-        return lax.psum(moved, "ctx").astype(f32)
-
-    sum_proj = owner(g_proj, 1, 0)
-    sum_fc = owner(g_fc, 0, 1)
-    sum_out = owner(g_out, 1, 0)
-    sum_qkv = owner(g_qkv, 1, 2)
+    early = all_to_all([g_proj.astype(bf), g_fc.astype(bf)], [(1, 0), (0, 1)], 5)
+
+    def line_sum(values):
+        part = lax.psum_scatter(values, "ctx", scatter_dimension=0, tiled=True)
+        return lax.all_gather(part, "ctx", axis=0, tiled=True).astype(f32)
+
+    sum_proj, sum_fc = line_sum(early[0]), line_sum(early[1])
+    late = all_to_all([g_out.astype(bf), g_qkv.astype(bf)], [(1, 0), (1, 2)], 6)
+    sum_out = lax.psum(late[0], "ctx").astype(f32)
+    sum_qkv = lax.psum(late[1], "ctx").astype(f32)
     col = t * b_qv.shape[1] + s * width
     g_bqv = jnp.stack([jnp.sum(d_query, axis=0), jnp.sum(d_value, axis=0)])
     full_bqv = lax.dynamic_update_slice(jnp.zeros((2, b_qv.shape[1] * cores), f32), g_bqv, (0, col))
@@ -444,7 +667,7 @@
             g_ln2b,
         ]
     )
-    packed = lax.psum(packed, ("shard", "ctx", "tp"))
+    packed = sum_everywhere(packed.reshape(-1, 128)).reshape(-1)
     at = full_bqv.size
     sum_bqv = lax.dynamic_slice_in_dim(
         packed[:at].reshape(full_bqv.shape), t * b_qv.shape[1], b_qv.shape[1], axis=1
@@ -505,7 +728,7 @@
         P(),
     )
     count = mesh.shape["shard"]
-    square = count == mesh.shape["ctx"] and count & (count - 1) == 0
+    square = count == mesh.shape["ctx"] and count & (count - 1) == 0 and mesh.shape["tp"] == 2
     body = on_device_plane if square else on_device_general
     return jax.shard_map(
         body, mesh=mesh, in_specs=in_specs, out_specs=out_specs, check_vma=False

time: 575 us -> 477 us (0.83)
  Pallas kernels: 0 us -> 284 us
  waiting for transfers between devices: 312 us -> 74.3 us
  starting transfers between devices: 76.4 us -> 7.5 us
  blocking collectives: 59.4 us -> 4.34 us
  local copies, waits for them, and re-layouts: 33.5 us -> 16.9 us
    pallas_call x0 -> x12, Pallas kernels: none -> 284 us  [comm_call(): pl.pallas_call(kernel, out_shape=out_shape, in_specs=[VMEM] * len(operand...]
    reduce_scatter x4 -> x2, waiting for transfers between devices: 129 us -> 0.02 us  [line_sum(): part = lax.psum_scatter(values, 'ctx', scatter_dimension=0, tiled=True)]
    ppermute x24 -> x0, starting transfers between devices: 71.2 us -> none  [exchange(): arrived.append((me ^ step, lax.ppermute(pieces_of(me ^ step), axis, pairs)))]
    psum x1, waiting for transfers between devices: 86.5 us -> 23.6 us  [on_device_plane(): sum_qkv = lax.psum(late[1], 'ctx').astype(f32)]
    psum x1 -> x0, blocking collectives: 55 us -> none  [on_device_plane(): packed = lax.psum(packed, ('shard', 'ctx', 'tp'))]
    ppermute x24 -> x0, waiting for transfers between devices: 43.3 us -> none  [exchange(): arrived.append((me ^ step, lax.ppermute(pieces_of(me ^ step), axis, pairs)))]
    dynamic_update_slice x24 -> x0, local copies, waits for them, and re-layouts: 9.86 us -> none  [place(): lax.dynamic_update_slice_in_dim(result, piece, index * depth, axis=concat)]
    all_gather x4 -> x2, waiting for transfers between devices: 53.7 us -> 50.6 us  [line_sum(): return lax.all_gather(part, 'ctx', axis=0, tiled=True).astype(f32)]
  transfers between devices with their start and end apart: 38 -> 10, of which waited for: 16 -> 3; matrix products, arithmetic and copies ran while one was open for 13% -> 13% of each run, Pallas kernels for 0% -> 46%
where the time goes in v2:
time: 477 us; the launch traced here: 475 us
  Pallas kernels  284 us (60%)
  waiting for transfers between devices  74.3 us (16%)
  matrix products  52 us (11%)
  other arithmetic  21.4 us (4%)
  local copies, waits for them, and re-layouts  16.9 us (4%)
  between operations  14.8 us (3%)
  starting transfers between devices  7.5 us (2%)
    pallas_call x12, Pallas kernels, comm_call(): pl.pallas_call(kernel, out_shape=out_shape, in_specs=[VMEM] * len(operand...  284 us
    all_gather x2, waiting for transfers between devices, line_sum(): return lax.all_gather(part, 'ctx', axis=0, tiled=True).astype(f32)  50.6 us
    psum x1, waiting for transfers between devices, on_device_plane(): sum_qkv = lax.psum(late[1], 'ctx').astype(f32)  23.6 us
    dot_general x10, matrix products, dot32(): return jnp.dot(left, right, preferred_element_type=jnp.float32)  15.9 us
    dot_general x6, matrix products, dot_t(): lax.dot_general(left, right, (((1,), (1,)), ((), ())), preferred_element_...  14 us
    dot_general x6, matrix products, t_dot(): lax.dot_general(left, right, (((0,), (0,)), ((), ())), preferred_element_...  10.5 us
  transfers between devices with their start and end apart: 10, of which 3 were waited for; matrix products, arithmetic and copies ran while one was open for 13% of the time, Pallas kernels for 46%

profile of v2, /device:TPU:0, one launch (start us, length us, event | category | flops | bytes accessed | tf_op | source)
XLA Modules:
  0.0 475.3 jit_solution(9941959804894542560)
XLA Ops:
  9.4 3.7 collective-permute-start.3
  16.2 62.2 %shard_map.255 = (bf16[3,1024,128]{2,1,0:T(8,128)(2,1)}, bf16[128,1024]{1,0:T(8,128)(2,1)}, bf16[1024,512]{1,0:T(8,128)(2,1)}, bf16[512,1024]{1,0:T(8,128)(2,1)}) custom-call(bf16[3,256,512]{2,1,0:T(8,128)(2,1)} %refs_0_.1, bf16[512,256]{1,0:T(8,128)(2,1)} %refs_1_.1, bf16[256,2048]{1,0:T(8,128)(2,1)} %refs_2_.1, bf16[2048,256]{1,0:T(8,128)(2,1)} %refs_3_.1), custom_call_target="tpu_custom_call" | custom-call | bytes 16777216 | tf_op jit(solution)/shard_map/pallas_call | solution.py:260
  80.1 19.7 %shard_map.254 = bf16[1024,1024]{1,0:T(8,128)(2,1)} custom-call(bf16[128,1024]{1,0:T(8,128)(2,1)} %fusion.51.x_ref), custom_call_target="tpu_custom_call" | custom-call | bytes 16777216 | tf_op jit(solution)/shard_map/pallas_call | solution.py:260
  111.2 19.2 %shard_map.256 = f32[128,1024]{1,0:T(8,128)} custom-call(bf16[1024,1024]{1,0:T(8,128)(2,1)} %convolution_convert_fusion.2.p_ref), custom_call_target="tpu_custom_call" | custom-call | bytes 16777216 | tf_op jit(solution)/shard_map/pallas_call | solution.py:260
  132.7 18.9 %shard_map.257 = bf16[1024,1024]{1,0:T(8,128)(2,1)} custom-call(bf16[128,1024]{1,0:T(8,128)(2,1)} %add_convert_fusion.2.x_ref), custom_call_target="tpu_custom_call" | custom-call | bytes 16777216 | tf_op jit(solution)/shard_map/pallas_call | solution.py:260
  151.6 4.4 fusion.123
  156.0 19.0 %shard_map.259 = bf16[1024,1024]{1,0:T(8,128)(2,1)} custom-call(bf16[128,1024]{1,0:T(8,128)(2,1)} %collective-permute-done.3.x_ref), custom_call_target="tpu_custom_call" | custom-call | bytes 16777216 | tf_op jit(solution)/shard_map/pallas_call | solution.py:260
  175.1 4.7 convolution_convert_fusion.4.refs_0_
  179.8 3.4 fusion.119
  183.3 2.8 convolution_convert_fusion.1.p_ref
  191.0 19.2 %shard_map.258 = f32[128,1024]{1,0:T(8,128)} custom-call(bf16[1024,1024]{1,0:T(8,128)(2,1)} %convolution_convert_fusion.1.p_ref), custom_call_target="tpu_custom_call" | custom-call | bytes 16777216 | tf_op jit(solution)/shard_map/pallas_call | solution.py:260
  210.3 28.3 %shard_map.264 = (bf16[2048,256]{1,0:T(8,128)(2,1)}, bf16[256,2048]{1,0:T(8,128)(2,1)}) custom-call(bf16[512,1024]{1,0:T(8,128)(2,1)} %convolution_convert_fusion.4.refs_0_, bf16[1024,512]{1,0:T(8,128)(2,1)} %convolution_convert_fusion.3.refs_1_), custom_call_target="tpu_custom_call" | custom-call | bytes 16777216 | tf_op jit(solution)/shard_map/pallas_call | solution.py:260
  238.7 18.9 %shard_map.260 = f32[128,1024]{1,0:T(8,128)} custom-call(bf16[1024,1024]{1,0:T(8,128)(2,1)} %convolution_convert_fusion.p_ref), custom_call_target="tpu_custom_call" | custom-call | bytes 16777216 | tf_op jit(solution)/shard_map/pallas_call | solution.py:260
  258.9 2.8 fusion.118
  263.2 18.9 %shard_map.261 = bf16[1024,1024]{1,0:T(8,128)(2,1)} custom-call(bf16[128,1024]{1,0:T(8,128)(2,1)} %convert_element_type.130.x_ref), custom_call_target="tpu_custom_call" | custom-call | bytes 16777216 | tf_op jit(solution)/shard_map/pallas_call | solution.py:260
  284.8 3.7 multiply_convert_fusion.1
  304.1 17.0 %shard_map.263 = (bf16[512,256]{1,0:T(8,128)(2,1)}, bf16[3,256,512]{2,1,0:T(8,128)(2,1)}) custom-call(bf16[128,1024]{1,0:T(8,128)(2,1)} %convolution_convert_fusion.8.refs_0_, bf16[3,1024,128]{2,1,0:T(8,128)(2,1)} %pad_maximum_fusion.refs_1_), custom_call_target="tpu_custom_call" | custom-call | bytes 16777216 | tf_op jit(solution)/shard_map/pallas_call | solution.py:260
  328.4 26.1 %shard_map.262 = f32[128,1024]{1,0:T(8,128)} custom-call(bf16[1024,1024]{1,0:T(8,128)(2,1)} %add_convert_fusion.p_ref), custom_call_target="tpu_custom_call" | custom-call | bytes 16777216 | tf_op jit(solution)/shard_map/pallas_call | solution.py:260
  357.2 16.7 %shard_map.265 = f32[96,128]{1,0:T(8,128)} custom-call(f32[96,128]{1,0:T(8,128)} %bitcast.71), custom_call_target="tpu_custom_call" | custom-call | bytes 4194304 | tf_op jit(solution)/shard_map/pallas_call | solution.py:260
  383.2 23.6 %all-reduce.3.cloned.1.call-done = (bf16[3,256,512]{2,1,0:T(8,128)(2,1)}, bf16[512,256]{1,0:T(8,128)(2,1)}) async-done(((bf16[3,256,512]{2,1,0:T(8,128)(2,1)}, bf16[512,256]{1,0:T(8,128)(2,1)}), (bf16[3,256,512]{2,1,0:T(8,128)(2,1)}, bf16[512,256]{1,0:T(8,128)(2,1)})) %all-reduce.3.cloned.1.call-update) | async-done | bytes 1048592 | tf_op jit(solution)/shard_map/psum | solution.py:651
  411.0 24.5 %all-gather.5.cloned.1.call-done = bf16[2048,256]{1,0:T(8,128)(2,1)} async-done(((bf16[512,256]{1,0:T(8,128)(2,1)}), bf16[2048,256]{1,0:T(8,128)(2,1)}) %all-gather.5.cloned.1.call-update) | async-done | bytes 1048592 | tf_op jit(solution)/shard_map/all_gather | solution.py:646
  435.6 2.8 convert_element_type.150
  438.3 26.0 %all-gather.3.cloned.1.call-done = bf16[256,2048]{1,0:T(8,128)(2,1)} async-done(((bf16[64,2048]{1,0:T(8,128)(2,1)}), bf16[256,2048]{1,0:T(8,128)(2,1)}) %all-gather.3.cloned.1.call-update) | async-done | bytes 1048592 | tf_op jit(solution)/shard_map/all_gather | solution.py:646
  464.4 2.8 convert_element_type.149
  (207 shorter events, 71.1 us)
Async XLA Ops:
  7.2 316.7 %reduce-scatter.5.cloned.1.call-start = ((), (), s32[]{:S(2)}) async-start(), calls=%async_computation.4 | async-start | bytes 1310720 | tf_op jit(solution)/shard_map/reduce_scatter | solution.py:645
  7.2 71.2 %collective-permute-start.1 = (s32[1,3]{1,0:T(1,128)}, s32[1,3]{1,0:T(1,128)S(1)}, u32[]{:S(2)}, u32[]{:S(2)}) collective-permute-start(s32[1,3]{1,0:T(1,128)} %param.16), channel_id=1, source_target_pairs={{0,0},{2,8},{4,16},{6,24},{8,2},{10,10},{12,18},{14,26},{16,4},{18... | collective-permute-start | bytes 44 | tf_op jit(solution)/shard_map/ppermute | solution.py:494
  9.4 69.7 %copy-start.33 = (f32[1024]{0:T(1024)S(1)}, f32[1024]{0:T(1024)}, u32[]{:S(2)}) copy-start(f32[1024]{0:T(1024)} %param.26) | copy-start | bytes 12292
  9.4 69.7 %copy-start.39 = (f32[1024]{0:T(1024)S(1)}, f32[1024]{0:T(1024)}, u32[]{:S(2)}) copy-start(f32[1024]{0:T(1024)} %param.27) | copy-start | bytes 12292
  9.4 146.6 %collective-permute-start.3 = (bf16[128,1024]{1,0:T(8,128)(2,1)}, bf16[128,1024]{1,0:T(8,128)(2,1)}, u32[]{:S(2)}, u32[]{:S(2)}) collective-permute-start(bf16[128,1024]{1,0:T(8,128)(2,1)} %constant_dynamic-slice_fusion.1), channel_id=1, source_target_pairs={{0,0},{2,8},{4,16},{6,24},{8,2},{10,10},{12,18},{14,26},{16,4},{18... | collective-permute-start | bytes 786440 | tf_op jit(solution)/shard_map/ppermute | solution.py:494
  14.1 64.6 %collective-permute-start = (bf16[128,1024]{1,0:T(8,128)(2,1)S(1)}, bf16[128,1024]{1,0:T(8,128)(2,1)S(1)}, u32[]{:S(2)}, u32[]{:S(2)}) collective-permute-start(bf16[128,1024]{1,0:T(8,128)(2,1)S(1)} %constant_dynamic-slice_fusion.3), channel_id=1, source_target_pairs={{0,0},{2,8},{4,16},{6,24},{8,2},{10,10},{12,18},{14,26},{16,4},{18... | collective-permute-start | bytes 786440 | tf_op jit(solution)/shard_map/ppermute | solution.py:494
  78.4 21.4 %copy-start.15 = (bf16[3,1024,128]{2,1,0:T(8,128)(2,1)S(1)}, bf16[3,1024,128]{2,1,0:T(8,128)(2,1)}, u32[]{:S(2)}) copy-start(bf16[3,1024,128]{2,1,0:T(8,128)(2,1)} %get-tuple-element.22) | copy-start | bytes 2359300
  78.7 206.0 %copy-start.43 = (s32[1024]{0:T(1024)}, s32[1024]{0:T(1024)S(1)}, u32[]{:S(2)}) copy-start(s32[1024]{0:T(1024)S(1)} %convert_reduce_fusion.2) | copy-start | bytes 12292
  78.9 23.5 %copy-start.35 = (f32[128]{0:T(128)}, f32[128]{0:T(128)S(1)}, u32[]{:S(2)}) copy-start(f32[128]{0:T(128)S(1)} %broadcast_multiply_fusion.5) | copy-start | bytes 1540
  79.1 23.3 %copy-start.37 = (f32[128]{0:T(128)}, f32[128]{0:T(128)S(1)}, u32[]{:S(2)}) copy-start(f32[128]{0:T(128)S(1)} %add_rsqrt_fusion.1) | copy-start | bytes 1540
  109.2 21.2 %copy-start.40 = (f32[1024]{0:T(1024)S(1)}, f32[1024]{0:T(1024)}, u32[]{:S(2)}) copy-start(f32[1024]{0:T(1024)} %param.23) | copy-start | bytes 12292
  111.2 20.6 %copy-start.41 = (f32[1024]{0:T(1024)S(1)}, f32[1024]{0:T(1024)}, u32[]{:S(2)}) copy-start(f32[1024]{0:T(1024)} %param.29) | copy-start | bytes 12292
  238.6 117.9 %reduce-scatter.3.cloned.1.call-start = ((), (), s32[]{:S(2)}) async-start(), calls=%async_computation.2 | async-start | bytes 1310720 | tf_op jit(solution)/shard_map/reduce_scatter | solution.py:645
  293.6 113.1 %all-reduce.3.cloned.1.call-start = ((), (), s32[]{:S(2)}) async-start(), calls=%async_computation.6 | async-start | bytes 2097152 | tf_op jit(solution)/shard_map/psum | solution.py:651
  321.1 114.5 %all-gather.5.cloned.1.call-start = ((), (), s32[]{:S(2)}) async-start(), calls=%async_computation.5 | async-start | bytes 1310720 | tf_op jit(solution)/shard_map/all_gather | solution.py:646
  323.9 140.5 %all-gather.3.cloned.1.call-start = ((), (), s32[]{:S(2)}) async-start(), calls=%async_computation.3 | async-start | bytes 1310720 | tf_op jit(solution)/shard_map/all_gather | solution.py:646
  324.9 54.0 %collective-permute-start.2 = (bf16[128,1024]{1,0:T(8,128)(2,1)S(1)}, bf16[128,1024]{1,0:T(8,128)(2,1)S(1)}, u32[]{:S(2)}, u32[]{:S(2)}) collective-permute-start(bf16[128,1024]{1,0:T(8,128)(2,1)S(1)} %copy-done.28), channel_id=1, source_target_pairs={{0,0},{2,8},{4,16},{6,24},{8,2},{10,10},{12,18},{14,26},{16,4},{18... | collective-permute-start | bytes 786440 | tf_op jit(solution)/shard_map/ppermute | solution.py:494
  328.3 26.2 %copy-start.48 = (f32[512]{0:T(512)S(1)}, f32[512]{0:T(512)}, u32[]{:S(2)}) copy-start(f32[512]{0:T(512)} %get-tuple-element.46) | copy-start | bytes 6148
  328.3 26.7 %copy-start.34 = (f32[1024]{0:T(1024)S(1)}, f32[1024]{0:T(1024)}, u32[]{:S(2)}) copy-start(f32[1024]{0:T(1024)} %get-tuple-element.44) | copy-start | bytes 12292
  328.4 26.8 %copy-start.36 = (f32[128]{0:T(128)S(1)}, f32[128]{0:T(128)}, u32[]{:S(2)}) copy-start(f32[128]{0:T(128)} %copy-done.35) | copy-start | bytes 1540
  328.4 26.8 %copy-start.38 = (f32[128]{0:T(128)S(1)}, f32[128]{0:T(128)}, u32[]{:S(2)}) copy-start(f32[128]{0:T(128)} %copy-done.37) | copy-start | bytes 1540
  328.4 45.6 %copy-start.11 = (f32[128,1024]{1,0:T(8,128)S(1)}, f32[128,1024]{1,0:T(8,128)}, u32[]{:S(2)}) copy-start(f32[128,1024]{1,0:T(8,128)} %copy-done.10) | copy-start | bytes 1572868
  374.2 6.8 %collective-permute-start.4 = (bf16[128,1024]{1,0:T(8,128)(2,1)S(1)}, bf16[128,1024]{1,0:T(8,128)(2,1)S(1)}, u32[]{:S(2)}, u32[]{:S(2)}) collective-permute-start(bf16[128,1024]{1,0:T(8,128)(2,1)S(1)} %fusion.56), channel_id=1, source_target_pairs={{0,0},{2,8},{4,16},{6,24},{8,2},{10,10},{12,18},{14,26},{16,4},{18... | collective-permute-start | bytes 786440 | tf_op jit(solution)/shard_map/ppermute | solution.py:494
  435.6 33.2 %copy-start.1 = (bf16[256,1024]{1,0:T(8,128)(2,1)S(1)}, bf16[256,1024]{1,0:T(8,128)(2,1)}, u32[]{:S(2)}) copy-start(bf16[256,1024]{1,0:T(8,128)(2,1)} %param.17) | copy-start | bytes 1572868
  (40 other events, 163.6 us)
Sparse Core Ops, SparseCore 0:
  238.7 26.4 reduce-scatter.4
  293.8 26.3 reduce-scatter.2
  322.6 84.0 all-reduce.2
  408.2 27.3 all-gather.4
  437.0 27.3 all-gather.2
